TPU v7x, 768 devices: a whole 4x8x12 slice. The times are simulated.
768 devices in a mesh: gx: 16 (over y, core), gy: 12 (over x, z_hi), gz: 4 (over z_lo).
Axes of the slice: x: 4, y: 8, z: 12 (z_hi: 3, z_lo: 4; z = z_hi * 4 + z_lo), core: 2. Of those that a mesh axis runs over, the one named last changes fastest.
Arguments:
- panels: bfloat16 [4, 4, 16, 96, 8192], P(None, None, 'gz', 'gy', 'gx'), may hold values from -6 to 6
- eof_basis: bfloat16 [4, 16, 10], replicated, may hold values from -1.5 to 1.5
- control: float32 [4, 10, 96, 8192], P(None, None, 'gy', ('gx', 'gz')), may hold values from -6 to 6
- coefficients: float32 [4, 96, 8192], P(None, 'gy', ('gx', 'gz')), may hold values from -0.5 to 1.6, as said below
Outputs:
- covariance_image: float32 [4, 10, 96, 8192], P(None, None, 'gy', ('gx', 'gz'))
Inputs may be any that keep to these rules, and one draw needn't show every extreme that they name: `coefficients`: kxx and kyy lie in 0.2 to 1, kxy = c sqrt(kxx kyy) with c in -0.5 to 0.5, and the inverse cell area lies in 0.6 to 1.6.
All inputs are finite; a program needn't handle non-finite values.
Results may differ from a plain program's by a relative error of at most 0.00085.
Values may be sent and summed in bfloat16 or wider, within the bound.
A program may use at most 32 MiB of HBM per device.

v0:
```python
import jax
import jax.numpy as jnp
from jax import lax
from jax.sharding import PartitionSpec as P

STEPS = 6


time_step = 0.09


def padded_2(cells, sides, width, closed):
    for axis, dim in sides:
        count = lax.axis_size(axis)
        ends = count if closed else count - 1
        head = lax.slice_in_dim(cells, 0, width, axis=dim)
        tail = lax.slice_in_dim(cells, cells.shape[dim] - width, cells.shape[dim], axis=dim)
        cells = jnp.concatenate(
            [
                lax.ppermute(tail, axis, [(i, (i + 1) % count) for i in range(ends)]),
                cells,
                lax.ppermute(head, axis, [((i + 1) % count, i) for i in range(ends)]),
            ],
            axis=dim,
        )
    return cells


def divergence(padded, coeffs):
    east_diff = padded[:, :-1, 1:] - padded[:, :-1, :-1]
    north_diff = padded[:, 1:, :-1] - padded[:, :-1, :-1]
    flux_east = coeffs[0, :-1, :-1] * east_diff + coeffs[1, :-1, :-1] * north_diff
    flux_north = coeffs[1, :-1, :-1] * east_diff + coeffs[2, :-1, :-1] * north_diff
    return (
        flux_east[:, 1:, 1:]
        - flux_east[:, 1:, :-1]
        + (flux_north[:, 1:, 1:] - flux_north[:, :-1, 1:])
    )


def forward_section(padded, coeffs):
    return padded[:, 1:-1, 1:-1] + time_step * coeffs[3, 1:-1, 1:-1] * divergence(padded, coeffs)


def adjoint_section(padded, coeffs):
    return padded[:, 1:-1, 1:-1] + time_step * divergence(coeffs[3] * padded, coeffs)


def extend(values, width):
    zonal_wide = padded_2(values, ((("gx", "gz"), 2),), width, True)
    return padded_2(zonal_wide, (("gy", 1),), width, False)


def diffuse(values, coeff_wide, halo_depth, section_fn):
    for outer_turn in range(STEPS // halo_depth):
        padded = extend(values, halo_depth)
        padded = section_fn(padded, coeff_wide)
        values = padded
    return values


def per_device(panels, eof_basis, control, coefficients):
    halo_depth = 1
    coeff_wide = extend(coefficients, halo_depth)
    members = panels.shape[0]
    fields, eof_count, row_count, col_count = control.shape
    flat_control = control.reshape(fields * eof_count, row_count, col_count)
    adjointed = diffuse(flat_control, coeff_wide, halo_depth, adjoint_section)
    projected = jnp.einsum(
        "mflyx,fle->mfeyx",
        lax.all_to_all(panels, "gz", split_axis=4, concat_axis=2, tiled=True),
        eof_basis,
        preferred_element_type=jnp.float32,
    )
    weights = adjointed.reshape(fields, eof_count, row_count, col_count)
    scores = jnp.sum(projected * weights[None], axis=(1, 2))
    combined = jnp.sum(projected * scores[:, None, None], axis=0) / (members - 1)
    result = diffuse(
        combined.reshape(fields * eof_count, row_count, col_count),
        coeff_wide,
        halo_depth,
        forward_section,
    )
    return result.reshape(fields, eof_count, row_count, col_count)


def solution(mesh):
    in_specs = (
        P(None, None, "gz", "gy", "gx"),
        P(),
        P(None, None, "gy", ("gx", "gz")),
        P(None, "gy", ("gx", "gz")),
    )
    out_specs = P(None, None, "gy", ("gx", "gz"))
    return jax.shard_map(
        per_device, mesh=mesh, in_specs=in_specs, out_specs=out_specs, check_vma=False
    )
```

profile of v0, /device:TPU:56, one launch (start us, length us, event | category | flops | bytes accessed | tf_op | source)
XLA Modules:
  0.0 426.9 jit_solution(13717089048126706654)
XLA Ops:
  21.2 10.6 %collective-permute-start.2 = (f32[4,1,130]{2,1,0:T(1,128)S(1)}, f32[4,1,130]{2,1,0:T(1,128)S(1)}, u32[]{:S(2)}, u32[]{:S(2)}) collective-permute-start(f32[4,1,130]{2,1,0:T(1,128)S(1)} %get-tuple-element.81), channel_id=1, source_target_pairs={{0,4},{4,8},{8,12},{12,16},{16,20},{20,24},{24,28},{28,32},{32,36}... | collective-permute-start | bytes 6248 | tf_op jit(solution)/shard_map/ppermute | solution.py:20
  34.5 8.5 %collective-permute-start.6 = (f32[40,1,130]{2,1,0:T(1,128)S(1)}, f32[40,1,130]{2,1,0:T(1,128)S(1)}, u32[]{:S(2)}, u32[]{:S(2)}) collective-permute-start(f32[40,1,130]{2,1,0:T(1,128)S(1)} %get-tuple-element.51), channel_id=1, source_target_pairs={{0,4},{4,8},{8,12},{12,16},{16,20},{20,24},{24,28},{28,32},{32,36}... | collective-permute-start | bytes 62408 | tf_op jit(solution)/shard_map/ppermute | solution.py:20
  45.8 7.1 %collective-permute-done.7 = f32[40,1,130]{2,1,0:T(1,128)S(1)} collective-permute-done((f32[40,1,130]{2,1,0:T(1,128)S(1)}, f32[40,1,130]{2,1,0:T(1,128)S(1)}, u32[]{:S(2)}, u32[]{:S(2)}) %collective-permute-start.7) | collective-permute-done | bytes 20832 | tf_op jit(solution)/shard_map/ppermute | solution.py:22
  67.2 7.1 %collective-permute-start.10 = (f32[40,1,130]{2,1,0:T(1,128)S(1)}, f32[40,1,130]{2,1,0:T(1,128)S(1)}, u32[]{:S(2)}, u32[]{:S(2)}) collective-permute-start(f32[40,1,130]{2,1,0:T(1,128)S(1)} %get-tuple-element.49), channel_id=1, source_target_pairs={{0,4},{4,8},{8,12},{12,16},{16,20},{20,24},{24,28},{28,32},{32,36}... | collective-permute-start | bytes 62408 | tf_op jit(solution)/shard_map/ppermute | solution.py:20
  76.0 8.3 %collective-permute-done.11 = f32[40,1,130]{2,1,0:T(1,128)S(1)} collective-permute-done((f32[40,1,130]{2,1,0:T(1,128)S(1)}, f32[40,1,130]{2,1,0:T(1,128)S(1)}, u32[]{:S(2)}, u32[]{:S(2)}) %collective-permute-start.11) | collective-permute-done | bytes 20832 | tf_op jit(solution)/shard_map/ppermute | solution.py:22
  102.2 8.1 %collective-permute-done.15 = f32[40,1,130]{2,1,0:T(1,128)S(1)} collective-permute-done((f32[40,1,130]{2,1,0:T(1,128)S(1)}, f32[40,1,130]{2,1,0:T(1,128)S(1)}, u32[]{:S(2)}, u32[]{:S(2)}) %collective-permute-start.15) | collective-permute-done | bytes 20832 | tf_op jit(solution)/shard_map/ppermute | solution.py:22
  122.7 6.8 %collective-permute-start.18 = (f32[40,1,130]{2,1,0:T(1,128)S(1)}, f32[40,1,130]{2,1,0:T(1,128)S(1)}, u32[]{:S(2)}, u32[]{:S(2)}) collective-permute-start(f32[40,1,130]{2,1,0:T(1,128)S(1)} %get-tuple-element.45), channel_id=1, source_target_pairs={{0,4},{4,8},{8,12},{12,16},{16,20},{20,24},{24,28},{28,32},{32,36}... | collective-permute-start | bytes 62408 | tf_op jit(solution)/shard_map/ppermute | solution.py:20
  131.2 8.1 %collective-permute-done.19 = f32[40,1,130]{2,1,0:T(1,128)S(1)} collective-permute-done((f32[40,1,130]{2,1,0:T(1,128)S(1)}, f32[40,1,130]{2,1,0:T(1,128)S(1)}, u32[]{:S(2)}, u32[]{:S(2)}) %collective-permute-start.19) | collective-permute-done | bytes 20832 | tf_op jit(solution)/shard_map/ppermute | solution.py:22
  142.3 7.5 %collective-permute-start.21 = (f32[40,8,1]{2,1,0:T(8,128)S(1)}, f32[40,8,1]{2,1,0:T(8,128)S(1)}, u32[]{:S(2)}, u32[]{:S(2)}) collective-permute-start(f32[40,8,1]{2,1,0:T(8,128)S(1)} %get-tuple-element.68), channel_id=1, source_target_pairs={{1,0},{2,1},{3,2},{48,3},{49,48},{50,49},{51,50},{96,51},{97,96},{... | collective-permute-start | bytes 3848 | tf_op jit(solution)/shard_map/ppermute | solution.py:22
  152.9 7.3 %collective-permute-start.22 = (f32[40,1,130]{2,1,0:T(1,128)S(1)}, f32[40,1,130]{2,1,0:T(1,128)S(1)}, u32[]{:S(2)}, u32[]{:S(2)}) collective-permute-start(f32[40,1,130]{2,1,0:T(1,128)S(1)} %get-tuple-element.43), channel_id=1, source_target_pairs={{0,4},{4,8},{8,12},{12,16},{16,20},{20,24},{24,28},{28,32},{32,36}... | collective-permute-start | bytes 62408 | tf_op jit(solution)/shard_map/ppermute | solution.py:20
  161.5 10.4 %copy.19 = bf16[4,4,4,8,512]{3,2,1,0,4:T(4,128)(2,1)} copy(bf16[4,4,4,8,512]{4,3,2,1,0:T(8,128)(2,1)S(1)} %copy-done) | data formatting | bytes 1048576 | tf_op args[0]
  171.9 11.3 %reshape.15 = bf16[4,2,32768]{2,1,0:T(2,128)(2,1)} reshape(bf16[512,4,4,4,8]{4,3,2,1,0:T(4,128)(2,1)} %bitcast.25) | data formatting | bytes 1048576
  196.0 7.4 %collective-permute-done.24 = f32[40,8,1]{2,1,0:T(8,128)S(1)} collective-permute-done((f32[40,8,1]{2,1,0:T(8,128)S(1)}, f32[40,8,1]{2,1,0:T(8,128)S(1)}, u32[]{:S(2)}, u32[]{:S(2)}) %collective-permute-start.24) | collective-permute-done | bytes 1312 | tf_op jit(solution)/shard_map/ppermute | solution.py:20
  203.8 7.8 %collective-permute-start.26 = (f32[40,1,130]{2,1,0:T(1,128)S(1)}, f32[40,1,130]{2,1,0:T(1,128)S(1)}, u32[]{:S(2)}, u32[]{:S(2)}) collective-permute-start(f32[40,1,130]{2,1,0:T(1,128)S(1)} %get-tuple-element.41), channel_id=1, source_target_pairs={{0,4},{4,8},{8,12},{12,16},{16,20},{20,24},{24,28},{28,32},{32,36}... | collective-permute-start | bytes 62408 | tf_op jit(solution)/shard_map/ppermute | solution.py:20
  213.2 8.1 %collective-permute-done.27 = f32[40,1,130]{2,1,0:T(1,128)S(1)} collective-permute-done((f32[40,1,130]{2,1,0:T(1,128)S(1)}, f32[40,1,130]{2,1,0:T(1,128)S(1)}, u32[]{:S(2)}, u32[]{:S(2)}) %collective-permute-start.27) | collective-permute-done | bytes 20832 | tf_op jit(solution)/shard_map/ppermute | solution.py:22
  222.4 11.1 %reshape.16 = bf16[512,4,4,4,8]{4,3,2,1,0:T(4,128)(2,1)} reshape(bf16[4,2,32768]{2,1,0:T(2,128)(2,1)S(1)} %all-to-all-done) | data formatting | bytes 1048576
  233.5 11.6 %copy.20 = bf16[4,4,4,8,4,128]{5,2,4,3,0,1:T(4,128)(2,1)S(1)} copy(bf16[4,4,4,8,4,128]{3,2,1,0,5,4:T(4,128)(2,1)} %bitcast.24) | data formatting | bytes 1048576 | tf_op jit(solution)/shard_map/all_to_all | solution.py:71
  245.7 7.2 %collective-permute-start.28 = (f32[40,8,1]{2,1,0:T(8,128)S(1)}, f32[40,8,1]{2,1,0:T(8,128)S(1)}, u32[]{:S(2)}, u32[]{:S(2)}) collective-permute-start(f32[40,8,1]{2,1,0:T(8,128)S(1)} %get-tuple-element.63), channel_id=1, source_target_pairs={{0,1},{1,2},{2,3},{3,48},{48,49},{49,50},{50,51},{51,96},{96,97},{... | collective-permute-start | bytes 3848 | tf_op jit(solution)/shard_map/ppermute | solution.py:20
  270.2 10.0 %collective-permute-done.31 = f32[40,1,130]{2,1,0:T(1,128)S(1)} collective-permute-done((f32[40,1,130]{2,1,0:T(1,128)S(1)}, f32[40,1,130]{2,1,0:T(1,128)S(1)}, u32[]{:S(2)}, u32[]{:S(2)}) %collective-permute-start.31) | collective-permute-done | bytes 20832 | tf_op jit(solution)/shard_map/ppermute | solution.py:22
  302.7 8.5 %collective-permute-done.35 = f32[40,1,130]{2,1,0:T(1,128)S(1)} collective-permute-done((f32[40,1,130]{2,1,0:T(1,128)S(1)}, f32[40,1,130]{2,1,0:T(1,128)S(1)}, u32[]{:S(2)}, u32[]{:S(2)}) %collective-permute-start.35) | collective-permute-done | bytes 20832 | tf_op jit(solution)/shard_map/ppermute | solution.py:22
  331.7 9.1 %collective-permute-done.39 = f32[40,1,130]{2,1,0:T(1,128)S(1)} collective-permute-done((f32[40,1,130]{2,1,0:T(1,128)S(1)}, f32[40,1,130]{2,1,0:T(1,128)S(1)}, u32[]{:S(2)}, u32[]{:S(2)}) %collective-permute-start.39) | collective-permute-done | bytes 20832 | tf_op jit(solution)/shard_map/ppermute | solution.py:22
  358.1 9.2 %collective-permute-done.43 = f32[40,1,130]{2,1,0:T(1,128)S(1)} collective-permute-done((f32[40,1,130]{2,1,0:T(1,128)S(1)}, f32[40,1,130]{2,1,0:T(1,128)S(1)}, u32[]{:S(2)}, u32[]{:S(2)}) %collective-permute-start.43) | collective-permute-done | bytes 20832 | tf_op jit(solution)/shard_map/ppermute | solution.py:22
  388.2 8.9 %collective-permute-done.47 = f32[40,1,130]{2,1,0:T(1,128)S(1)} collective-permute-done((f32[40,1,130]{2,1,0:T(1,128)S(1)}, f32[40,1,130]{2,1,0:T(1,128)S(1)}, u32[]{:S(2)}, u32[]{:S(2)}) %collective-permute-start.47) | collective-permute-done | bytes 20832 | tf_op jit(solution)/shard_map/ppermute | solution.py:22
  417.1 8.5 %collective-permute-done.51 = f32[40,1,130]{2,1,0:T(1,128)S(1)} collective-permute-done((f32[40,1,130]{2,1,0:T(1,128)S(1)}, f32[40,1,130]{2,1,0:T(1,128)S(1)}, u32[]{:S(2)}, u32[]{:S(2)}) %collective-permute-start.51) | collective-permute-done | bytes 20832 | tf_op jit(solution)/shard_map/ppermute | solution.py:22
  (159 shorter events, 217.5 us)
Async XLA Ops:
  0.9 19.4 %collective-permute-start = (f32[4,8,1]{2,1,0:T(8,128)S(1)}, f32[4,8,1]{2,1,0:T(8,128)S(1)}, u32[]{:S(2)}, u32[]{:S(2)}) collective-permute-start(f32[4,8,1]{2,1,0:T(8,128)S(1)} %get-tuple-element.82), channel_id=1, source_target_pairs={{0,1},{1,2},{2,3},{3,48},{48,49},{49,50},{50,51},{51,96},{96,97},{... | collective-permute-start | bytes 392 | tf_op jit(solution)/shard_map/ppermute | solution.py:20
  5.1 15.2 %collective-permute-start.1 = (f32[4,8,1]{2,1,0:T(8,128)S(1)}, f32[4,8,1]{2,1,0:T(8,128)S(1)}, u32[]{:S(2)}, u32[]{:S(2)}) collective-permute-start(f32[4,8,1]{2,1,0:T(8,128)S(1)} %get-tuple-element.83), channel_id=1, source_target_pairs={{1,0},{2,1},{3,2},{48,3},{49,48},{50,49},{51,50},{96,51},{97,96},{... | collective-permute-start | bytes 392 | tf_op jit(solution)/shard_map/ppermute | solution.py:22
  12.0 21.1 %collective-permute-start.4 = (f32[40,8,1]{2,1,0:T(8,128)S(1)}, f32[40,8,1]{2,1,0:T(8,128)S(1)}, u32[]{:S(2)}, u32[]{:S(2)}) collective-permute-start(f32[40,8,1]{2,1,0:T(8,128)S(1)} %get-tuple-element.75), channel_id=1, source_target_pairs={{0,1},{1,2},{2,3},{3,48},{48,49},{49,50},{50,51},{51,96},{96,97},{... | collective-permute-start | bytes 3848 | tf_op jit(solution)/shard_map/ppermute | solution.py:20
  13.9 19.2 %collective-permute-start.5 = (f32[40,8,1]{2,1,0:T(8,128)S(1)}, f32[40,8,1]{2,1,0:T(8,128)S(1)}, u32[]{:S(2)}, u32[]{:S(2)}) collective-permute-start(f32[40,8,1]{2,1,0:T(8,128)S(1)} %get-tuple-element.76), channel_id=1, source_target_pairs={{1,0},{2,1},{3,2},{48,3},{49,48},{50,49},{51,50},{96,51},{97,96},{... | collective-permute-start | bytes 3848 | tf_op jit(solution)/shard_map/ppermute | solution.py:22
  21.2 23.0 %collective-permute-start.2 = (f32[4,1,130]{2,1,0:T(1,128)S(1)}, f32[4,1,130]{2,1,0:T(1,128)S(1)}, u32[]{:S(2)}, u32[]{:S(2)}) collective-permute-start(f32[4,1,130]{2,1,0:T(1,128)S(1)} %get-tuple-element.81), channel_id=1, source_target_pairs={{0,4},{4,8},{8,12},{12,16},{16,20},{20,24},{24,28},{28,32},{32,36}... | collective-permute-start | bytes 6248 | tf_op jit(solution)/shard_map/ppermute | solution.py:20
  31.8 13.2 %collective-permute-start.3 = (f32[4,1,130]{2,1,0:T(1,128)S(1)}, f32[4,1,130]{2,1,0:T(1,128)S(1)}, u32[]{:S(2)}, u32[]{:S(2)}) collective-permute-start(f32[4,1,130]{2,1,0:T(1,128)S(1)} %get-tuple-element.80), channel_id=1, source_target_pairs={{4,0},{8,4},{12,8},{16,12},{20,16},{24,20},{28,24},{32,28},{36,32}... | collective-permute-start | bytes 6248 | tf_op jit(solution)/shard_map/ppermute | solution.py:22
  34.5 11.4 %collective-permute-start.6 = (f32[40,1,130]{2,1,0:T(1,128)S(1)}, f32[40,1,130]{2,1,0:T(1,128)S(1)}, u32[]{:S(2)}, u32[]{:S(2)}) collective-permute-start(f32[40,1,130]{2,1,0:T(1,128)S(1)} %get-tuple-element.51), channel_id=1, source_target_pairs={{0,4},{4,8},{8,12},{12,16},{16,20},{20,24},{24,28},{28,32},{32,36}... | collective-permute-start | bytes 62408 | tf_op jit(solution)/shard_map/ppermute | solution.py:20
  55.8 10.8 %collective-permute-start.8 = (f32[40,8,1]{2,1,0:T(8,128)S(1)}, f32[40,8,1]{2,1,0:T(8,128)S(1)}, u32[]{:S(2)}, u32[]{:S(2)}) collective-permute-start(f32[40,8,1]{2,1,0:T(8,128)S(1)} %get-tuple-element.73), channel_id=1, source_target_pairs={{0,1},{1,2},{2,3},{3,48},{48,49},{49,50},{50,51},{51,96},{96,97},{... | collective-permute-start | bytes 3848 | tf_op jit(solution)/shard_map/ppermute | solution.py:20
  140.3 11.4 %collective-permute-start.20 = (f32[40,8,1]{2,1,0:T(8,128)S(1)}, f32[40,8,1]{2,1,0:T(8,128)S(1)}, u32[]{:S(2)}, u32[]{:S(2)}) collective-permute-start(f32[40,8,1]{2,1,0:T(8,128)S(1)} %get-tuple-element.67), channel_id=1, source_target_pairs={{0,1},{1,2},{2,3},{3,48},{48,49},{49,50},{50,51},{51,96},{96,97},{... | collective-permute-start | bytes 3848 | tf_op jit(solution)/shard_map/ppermute | solution.py:20
  142.3 10.3 %collective-permute-start.21 = (f32[40,8,1]{2,1,0:T(8,128)S(1)}, f32[40,8,1]{2,1,0:T(8,128)S(1)}, u32[]{:S(2)}, u32[]{:S(2)}) collective-permute-start(f32[40,8,1]{2,1,0:T(8,128)S(1)} %get-tuple-element.68), channel_id=1, source_target_pairs={{1,0},{2,1},{3,2},{48,3},{49,48},{50,49},{51,50},{96,51},{97,96},{... | collective-permute-start | bytes 3848 | tf_op jit(solution)/shard_map/ppermute | solution.py:22
  152.9 33.8 %collective-permute-start.22 = (f32[40,1,130]{2,1,0:T(1,128)S(1)}, f32[40,1,130]{2,1,0:T(1,128)S(1)}, u32[]{:S(2)}, u32[]{:S(2)}) collective-permute-start(f32[40,1,130]{2,1,0:T(1,128)S(1)} %get-tuple-element.43), channel_id=1, source_target_pairs={{0,4},{4,8},{8,12},{12,16},{16,20},{20,24},{24,28},{28,32},{32,36}... | collective-permute-start | bytes 62408 | tf_op jit(solution)/shard_map/ppermute | solution.py:20
  160.2 26.5 %collective-permute-start.23 = (f32[40,1,130]{2,1,0:T(1,128)S(1)}, f32[40,1,130]{2,1,0:T(1,128)S(1)}, u32[]{:S(2)}, u32[]{:S(2)}) collective-permute-start(f32[40,1,130]{2,1,0:T(1,128)S(1)} %get-tuple-element.44), channel_id=1, source_target_pairs={{4,0},{8,4},{12,8},{16,12},{20,16},{24,20},{28,24},{32,28},{36,32}... | collective-permute-start | bytes 62408 | tf_op jit(solution)/shard_map/ppermute | solution.py:22
  183.2 39.1 %all-to-all-start = ((bf16[4,2,32768]{2,1,0:T(2,128)(2,1)}), bf16[4,2,32768]{2,1,0:T(2,128)(2,1)S(1)}, u32[]{:S(2)}, u32[]{:S(2)}) async-start(bf16[4,2,32768]{2,1,0:T(2,128)(2,1)} %reshape.15), calls=%async_computation | async-start | bytes 1048576 | tf_op jit(solution)/shard_map/all_to_all | solution.py:71
  187.7 15.7 %collective-permute-start.24 = (f32[40,8,1]{2,1,0:T(8,128)S(1)}, f32[40,8,1]{2,1,0:T(8,128)S(1)}, u32[]{:S(2)}, u32[]{:S(2)}) collective-permute-start(f32[40,8,1]{2,1,0:T(8,128)S(1)} %get-tuple-element.65), channel_id=1, source_target_pairs={{0,1},{1,2},{2,3},{3,48},{48,49},{49,50},{50,51},{51,96},{96,97},{... | collective-permute-start | bytes 3848 | tf_op jit(solution)/shard_map/ppermute | solution.py:20
  191.6 11.8 %collective-permute-start.25 = (f32[40,8,1]{2,1,0:T(8,128)S(1)}, f32[40,8,1]{2,1,0:T(8,128)S(1)}, u32[]{:S(2)}, u32[]{:S(2)}) collective-permute-start(f32[40,8,1]{2,1,0:T(8,128)S(1)} %get-tuple-element.66), channel_id=1, source_target_pairs={{1,0},{2,1},{3,2},{48,3},{49,48},{50,49},{51,50},{96,51},{97,96},{... | collective-permute-start | bytes 3848 | tf_op jit(solution)/shard_map/ppermute | solution.py:22
  245.7 11.1 %collective-permute-start.28 = (f32[40,8,1]{2,1,0:T(8,128)S(1)}, f32[40,8,1]{2,1,0:T(8,128)S(1)}, u32[]{:S(2)}, u32[]{:S(2)}) collective-permute-start(f32[40,8,1]{2,1,0:T(8,128)S(1)} %get-tuple-element.63), channel_id=1, source_target_pairs={{0,1},{1,2},{2,3},{3,48},{48,49},{49,50},{50,51},{51,96},{96,97},{... | collective-permute-start | bytes 3848 | tf_op jit(solution)/shard_map/ppermute | solution.py:20
  252.8 10.3 %collective-permute-start.29 = (f32[40,8,1]{2,1,0:T(8,128)S(1)}, f32[40,8,1]{2,1,0:T(8,128)S(1)}, u32[]{:S(2)}, u32[]{:S(2)}) collective-permute-start(f32[40,8,1]{2,1,0:T(8,128)S(1)} %get-tuple-element.64), channel_id=1, source_target_pairs={{1,0},{2,1},{3,2},{48,3},{49,48},{50,49},{51,50},{96,51},{97,96},{... | collective-permute-start | bytes 3848 | tf_op jit(solution)/shard_map/ppermute | solution.py:22
  268.5 11.6 %collective-permute-start.31 = (f32[40,1,130]{2,1,0:T(1,128)S(1)}, f32[40,1,130]{2,1,0:T(1,128)S(1)}, u32[]{:S(2)}, u32[]{:S(2)}) collective-permute-start(f32[40,1,130]{2,1,0:T(1,128)S(1)} %get-tuple-element.39), channel_id=1, source_target_pairs={{4,0},{8,4},{12,8},{16,12},{20,16},{24,20},{28,24},{32,28},{36,32}... | collective-permute-start | bytes 62408 | tf_op jit(solution)/shard_map/ppermute | solution.py:22
  282.7 11.1 %collective-permute-start.33 = (f32[40,8,1]{2,1,0:T(8,128)S(1)}, f32[40,8,1]{2,1,0:T(8,128)S(1)}, u32[]{:S(2)}, u32[]{:S(2)}) collective-permute-start(f32[40,8,1]{2,1,0:T(8,128)S(1)} %get-tuple-element.62), channel_id=1, source_target_pairs={{1,0},{2,1},{3,2},{48,3},{49,48},{50,49},{51,50},{96,51},{97,96},{... | collective-permute-start | bytes 3848 | tf_op jit(solution)/shard_map/ppermute | solution.py:22
  300.2 11.0 %collective-permute-start.35 = (f32[40,1,130]{2,1,0:T(1,128)S(1)}, f32[40,1,130]{2,1,0:T(1,128)S(1)}, u32[]{:S(2)}, u32[]{:S(2)}) collective-permute-start(f32[40,1,130]{2,1,0:T(1,128)S(1)} %get-tuple-element.37), channel_id=1, source_target_pairs={{4,0},{8,4},{12,8},{16,12},{20,16},{24,20},{28,24},{32,28},{36,32}... | collective-permute-start | bytes 62408 | tf_op jit(solution)/shard_map/ppermute | solution.py:22
  329.4 11.5 %collective-permute-start.39 = (f32[40,1,130]{2,1,0:T(1,128)S(1)}, f32[40,1,130]{2,1,0:T(1,128)S(1)}, u32[]{:S(2)}, u32[]{:S(2)}) collective-permute-start(f32[40,1,130]{2,1,0:T(1,128)S(1)} %get-tuple-element.35), channel_id=1, source_target_pairs={{4,0},{8,4},{12,8},{16,12},{20,16},{24,20},{28,24},{32,28},{36,32}... | collective-permute-start | bytes 62408 | tf_op jit(solution)/shard_map/ppermute | solution.py:22
  356.1 11.2 %collective-permute-start.43 = (f32[40,1,130]{2,1,0:T(1,128)S(1)}, f32[40,1,130]{2,1,0:T(1,128)S(1)}, u32[]{:S(2)}, u32[]{:S(2)}) collective-permute-start(f32[40,1,130]{2,1,0:T(1,128)S(1)} %get-tuple-element.33), channel_id=1, source_target_pairs={{4,0},{8,4},{12,8},{16,12},{20,16},{24,20},{28,24},{32,28},{36,32}... | collective-permute-start | bytes 62408 | tf_op jit(solution)/shard_map/ppermute | solution.py:22
  386.2 10.9 %collective-permute-start.47 = (f32[40,1,130]{2,1,0:T(1,128)S(1)}, f32[40,1,130]{2,1,0:T(1,128)S(1)}, u32[]{:S(2)}, u32[]{:S(2)}) collective-permute-start(f32[40,1,130]{2,1,0:T(1,128)S(1)} %get-tuple-element.31), channel_id=1, source_target_pairs={{4,0},{8,4},{12,8},{16,12},{20,16},{24,20},{28,24},{32,28},{36,32}... | collective-permute-start | bytes 62408 | tf_op jit(solution)/shard_map/ppermute | solution.py:22
  415.0 10.5 %collective-permute-start.51 = (f32[40,1,130]{2,1,0:T(1,128)S(1)}, f32[40,1,130]{2,1,0:T(1,128)S(1)}, u32[]{:S(2)}, u32[]{:S(2)}) collective-permute-start(f32[40,1,130]{2,1,0:T(1,128)S(1)} %get-tuple-element.29), channel_id=1, source_target_pairs={{4,0},{8,4},{12,8},{16,12},{20,16},{24,20},{28,24},{32,28},{36,32}... | collective-permute-start | bytes 62408 | tf_op jit(solution)/shard_map/ppermute | solution.py:22
  (31 other events, 354.3 us)
where the time goes:
time: 432 us; the launch traced here: 427 us
  starting transfers between devices  214 us (50%)
  waiting for transfers between devices  142 us (33%)
  local copies, waits for them, and re-layouts  47.5 us (11%)
  other arithmetic  21.6 us (5%)
    ppermute x26, starting transfers between devices, padded_2(): lax.ppermute(tail, axis, [(i, (i + 1) % count) for i in range(ends)])  118 us
    ppermute x26, waiting for transfers between devices, padded_2(): lax.ppermute(head, axis, [((i + 1) % count, i) for i in range(ends)])  115 us
    ppermute x26, starting transfers between devices, padded_2(): lax.ppermute(head, axis, [((i + 1) % count, i) for i in range(ends)])  92.5 us
    unnamed x7, local copies, waits for them, and re-layouts  32.9 us
    ppermute x26, waiting for transfers between devices, padded_2(): lax.ppermute(tail, axis, [(i, (i + 1) % count) for i in range(ends)])  27.2 us
    all_to_all x1, local copies, waits for them, and re-layouts, per_device(): lax.all_to_all(panels, 'gz', split_axis=4, concat_axis=2, tiled=True)  11.6 us
  transfers between devices with their start and end apart: 53, of which 41 were waited for; matrix products, arithmetic and copies ran while one was open for 7% of the time, Pallas kernels for 0%

commit v1 on v0

v1 whole, which is shorter than its diff:
```python
import functools

import jax
import jax.numpy as jnp
from jax import lax
from jax.experimental import pallas as pl
from jax.experimental.pallas import tpu as pltpu
from jax.sharding import PartitionSpec as P

STEPS = 6
TIME_STEP = 0.09
ROWS = 8
COLS = 128
DEPTH = STEPS
EXT = ROWS + 2 * DEPTH
SLOT = COLS // ROWS
PLANES = 40
WIDE = 48
MESH = pl.DeviceIdType.MESH


def adjoint_steps(grid, coef):
    def one_step(_, carry):
        def weighted(r):
            return coef[r, 3][None] * grid[r]

        below = None
        here = weighted(0)
        for r in range(EXT - 1):
            above = weighted(r + 1)
            east = pltpu.roll(here, 2 * COLS - 1, 2) - here
            north = above - here
            kxy = coef[r, 1][None]
            flux_north = kxy * east + coef[r, 2][None] * north
            if r > 0:
                flux_east = coef[r, 0][None] * east + kxy * north
                grid[r] = grid[r] + (
                    (flux_east - pltpu.roll(flux_east, 1, 2)) + (flux_north - below)
                )
            below = flux_north
            here = above
        return carry

    lax.fori_loop(0, STEPS, one_step, 0)


def forward_steps(grid, coef):
    def one_step(_, carry):
        below = None
        here = grid[0]
        for r in range(EXT - 1):
            above = grid[r + 1]
            east = pltpu.roll(here, 2 * COLS - 1, 2) - here
            north = above - here
            kxy = coef[r, 1][None]
            flux_north = kxy * east + coef[r, 2][None] * north
            if r > 0:
                flux_east = coef[r, 0][None] * east + kxy * north
                grid[r] = here + coef[r, 3][None] * (
                    (flux_east - pltpu.roll(flux_east, 1, 2)) + (flux_north - below)
                )
            below = flux_north
            here = above
        return carry

    lax.fori_loop(0, STEPS, one_step, 0)


def kernel(
    sizes,
    panels_hbm,
    eof_hbm,
    control_hbm,
    coef_hbm,
    out_ref,
    control,
    coef_in,
    eof,
    panel,
    weight,
    projected,
    grid,
    coef,
    tile_a,
    edge_a,
    north_a,
    south_a,
    side_a,
    tile_b,
    edge_b,
    north_b,
    south_b,
    side_b,
    local_sem,
    send_sem,
    recv_sem,
):
    count_x, count_y, count_z = sizes
    gx, gy, gz = lax.axis_index("gx"), lax.axis_index("gy"), lax.axis_index("gz")
    place = gx * count_z + gz
    total = count_x * count_z
    east = lax.rem(place + 1, total)
    west = lax.rem(place + total - 1, total)
    up = lax.rem(gy + 1, count_y)
    down = lax.rem(gy + count_y - 1, count_y)

    def at(column, row):
        return (column // count_z, row, lax.rem(column, count_z))

    sides = [at(east, gy), at(west, gy), at(east, up), at(west, up), at(east, down), at(west, down)]
    peers = [(gx, gy, lax.rem(gz + d, count_z)) for d in range(1, count_z)]
    north_id, south_id = at(place, up), at(place, down)

    copies = [
        pltpu.make_async_copy(control_hbm, control, local_sem.at[0]),
        pltpu.make_async_copy(coef_hbm, coef_in.at[pl.ds(0, 32)], local_sem.at[1]),
        pltpu.make_async_copy(coef_hbm, coef_in.at[pl.ds(32, 32)], local_sem.at[2]),
        pltpu.make_async_copy(eof_hbm, eof, local_sem.at[3]),
    ]
    for copy in copies:
        copy.start()

    levels = panel.shape[1] // count_z
    mine = pl.ds(pl.multiple_of(gz * levels, levels), levels)
    own_panel = pltpu.make_async_copy(
        panels_hbm.at[:, :, pl.ds(pl.multiple_of(gz * COLS, COLS), COLS)],
        panel.at[:, mine, :],
        local_sem.at[4],
    )
    own_panel.start()

    barrier = pltpu.get_barrier_semaphore()
    partners = sides + [north_id, south_id] + peers
    for partner in partners:
        pl.semaphore_signal(barrier, inc=1, device_id=partner, device_id_type=MESH)

    lane = lax.broadcasted_iota(jnp.int32, (WIDE, COLS), 1)
    sub8 = lax.broadcasted_iota(jnp.int32, (8, COLS), 0)
    for copy in copies[:3]:
        copy.wait()

    edge = jnp.zeros((WIDE, COLS), jnp.float32)
    for y in range(ROWS):
        fields = control[pl.ds(y, PLANES, stride=ROWS), :]
        grid[DEPTH + y, :, :, 0:COLS] = fields.reshape(5, 8, COLS)
        entries = coef_in[pl.ds(y, 8, stride=ROWS), :]
        for k in range(4):
            scale = TIME_STEP if k == 3 else 1.0
            coef[DEPTH + y, k, :, 0:COLS] = jnp.broadcast_to(scale * entries[k : k + 1], (8, COLS))
        high = entries.astype(jnp.bfloat16).astype(jnp.float32)
        row = jnp.concatenate([fields, jnp.where(sub8 < 4, high, entries - high)], axis=0)
        tile_a[y] = row.astype(jnp.bfloat16)
        shifted = pltpu.roll(row, SLOT * y + SLOT // 2, 1)
        edge = jnp.where((lane >= SLOT * y) & (lane < SLOT * (y + 1)), shifted, edge)
    edge_a[...] = edge.astype(jnp.bfloat16)

    def exchange(first, tile, edge, north, south, side):
        moves = [(edge, side.at[k], sides[k]) for k in range(6)]
        moves = [
            (tile.at[pl.ds(ROWS - DEPTH, DEPTH)], south, north_id),
            (tile.at[pl.ds(0, DEPTH)], north, south_id),
        ] + moves
        return [
            pltpu.make_async_remote_copy(
                src_ref=source,
                dst_ref=target,
                send_sem=send_sem.at[first + k],
                recv_sem=recv_sem.at[first + k],
                device_id=device,
                device_id_type=MESH,
            )
            for k, (source, target, device) in enumerate(moves)
        ]

    pl.semaphore_wait(barrier, len(partners))
    halo_a = exchange(0, tile_a, edge_a, north_a, south_a, side_a)
    for copy in halo_a:
        copy.start()
    sent_panels = []
    for d in range(1, count_z):
        peer = lax.rem(gz + d, count_z)
        copy = pltpu.make_async_remote_copy(
            src_ref=panels_hbm.at[:, :, pl.ds(pl.multiple_of(peer * COLS, COLS), COLS)],
            dst_ref=panel.at[:, mine, :],
            send_sem=send_sem.at[16 + d],
            recv_sem=recv_sem.at[16 + d],
            device_id=peers[d - 1],
            device_id_type=MESH,
        )
        copy.start()
        sent_panels.append(copy)

    copies[3].wait()
    plane_of = lax.broadcasted_iota(jnp.int32, (PLANES, 10), 0)
    eof_of = lax.broadcasted_iota(jnp.int32, (PLANES, 10), 1)

    def field_of(plane):
        one = jnp.ones_like(plane)
        none = jnp.zeros_like(plane)
        found = jnp.where(plane >= 10, one, none)
        found = found + jnp.where(plane >= 20, one, none)
        return found + jnp.where(plane >= 30, one, none)

    pick = jnp.where(plane_of - 10 * field_of(plane_of) == eof_of, 1.0, 0.0).astype(jnp.bfloat16)
    by_plane = lax.dot_general(
        pick, eof[...], (((1,), (1,)), ((), ())), preferred_element_type=jnp.float32
    )
    plane_row = lax.broadcasted_iota(jnp.int32, (PLANES, 64), 0)
    level_col = lax.broadcasted_iota(jnp.int32, (PLANES, 64), 1)
    by_plane = jnp.where(field_of(plane_row) == lax.shift_right_logical(level_col, 4), by_plane, 0.0)
    level_row = lax.broadcasted_iota(jnp.int32, (64, 512), 0)
    spot = lax.broadcasted_iota(jnp.int32, (64, 512), 1)
    source = lax.shift_right_logical(spot, 7)
    field = lax.shift_right_logical(spot, 5) & 3
    level = lax.shift_right_logical(spot, 3) & 3
    repeat = jnp.where(level_row == field * 16 + source * 4 + level, 1.0, 0.0).astype(jnp.bfloat16)
    spread = jnp.dot(by_plane.astype(jnp.bfloat16), repeat, preferred_element_type=jnp.float32)
    spread_row = lax.broadcasted_iota(jnp.int32, (PLANES, 512), 1) & 7
    for pair in range(ROWS // 2):
        both = [jnp.where(spread_row == 2 * pair + k, spread, 0.0) for k in range(2)]
        weight[pl.ds(2 * PLANES * pair, 2 * PLANES), :] = jnp.concatenate(both, axis=0).astype(jnp.bfloat16)

    keep_north = jnp.where(gy < count_y - 1, 1.0, 0.0).astype(jnp.float32)
    keep_south = jnp.where(gy > 0, 1.0, 0.0).astype(jnp.float32)

    def halo_rows(north, south, side, planes):
        from_west = (lax.broadcasted_iota(jnp.int32, (planes, COLS), 1) & (SLOT - 1)) < SLOT // 2

        def edges(a, b):
            return jnp.where(
                from_west, side[a].astype(jnp.float32), side[b].astype(jnp.float32)
            )

        def slot(pack, y):
            return pltpu.roll(pack, COLS - SLOT // 2 - SLOT * y, 1)

        pack = edges(0, 1)
        for y in range(ROWS):
            yield DEPTH + y, None, slot(pack, y)
        pack = edges(2, 3) * keep_south
        for y in range(DEPTH):
            block = south[y].astype(jnp.float32) * keep_south
            yield y, block, slot(pack, y + ROWS - DEPTH)
        pack = edges(4, 5) * keep_north
        for y in range(DEPTH):
            block = north[y].astype(jnp.float32) * keep_north
            yield DEPTH + ROWS + y, block, slot(pack, y)

    def put(row, start, block):
        columns = slice(start, start + COLS)
        grid[row, :, :, columns] = block[0:PLANES].reshape(5, 8, COLS)

    def put_coef(row, start, block):
        parts = block[PLANES:WIDE]
        entries = parts + pltpu.roll(parts, 4, 0)
        for k in range(4):
            scale = TIME_STEP if k == 3 else 1.0
            coef[row, k, :, start : start + COLS] = jnp.broadcast_to(
                scale * entries[k : k + 1], (8, COLS)
            )

    for copy in halo_a:
        copy.wait_recv()
    for row, block, side in halo_rows(north_a, south_a, side_a, WIDE):
        if block is not None:
            put(row, 0, block)
            put_coef(row, 0, block)
        put(row, COLS, side)
        put_coef(row, COLS, side)
    adjoint_steps(grid, coef)

    own_panel.wait()
    for copy in sent_panels:
        copy.wait_recv()
    members = panel.shape[0]
    for m in range(0, members, 2):
        pair = jnp.concatenate([panel[m], panel[m + 1]], axis=1)
        projected[:, m * COLS : (m + 2) * COLS] = jnp.dot(
            weight[...], pair, preferred_element_type=jnp.float32
        )

    edge = jnp.zeros((PLANES, COLS), jnp.float32)
    lane = lax.broadcasted_iota(jnp.int32, (PLANES, COLS), 1)
    for y in range(ROWS):
        factor = grid[DEPTH + y, :, :, 0:COLS].reshape(PLANES, COLS)
        row = None
        for m in range(members):
            term = projected[y * PLANES : (y + 1) * PLANES, m * COLS : (m + 1) * COLS]
            score = jnp.sum(term * factor, axis=0, keepdims=True) * (1.0 / (members - 1))
            row = term * score if row is None else row + term * score
        grid[DEPTH + y, :, :, 0:COLS] = row.reshape(5, 8, COLS)
        tile_b[y] = row.astype(jnp.bfloat16)
        shifted = pltpu.roll(row, SLOT * y + SLOT // 2, 1)
        edge = jnp.where((lane >= SLOT * y) & (lane < SLOT * (y + 1)), shifted, edge)
    edge_b[...] = edge.astype(jnp.bfloat16)

    halo_b = exchange(8, tile_b, edge_b, north_b, south_b, side_b)
    for copy in halo_b:
        copy.start()
    for copy in halo_b:
        copy.wait_recv()
    for row, block, side in halo_rows(north_b, south_b, side_b, PLANES):
        if block is not None:
            put(row, 0, block)
        put(row, COLS, side)
    forward_steps(grid, coef)

    for y in range(ROWS):
        out_ref[pl.ds(y, PLANES, stride=ROWS), :] = grid[DEPTH + y, :, :, 0:COLS].reshape(PLANES, COLS)
    for copy in halo_a + sent_panels + halo_b:
        copy.wait_send()


def solution(mesh):
    sizes = tuple(mesh.shape[name] for name in ("gx", "gy", "gz"))

    def per_device(panels, eof_basis, control, coefficients):
        members, fields, levels, rows, columns = panels.shape
        eof_count = eof_basis.shape[2]
        deep = fields * levels * rows
        f32, bf16 = jnp.float32, jnp.bfloat16
        anywhere = pl.BlockSpec(memory_space=pl.ANY)
        out = pl.pallas_call(
            functools.partial(kernel, sizes),
            out_shape=jax.ShapeDtypeStruct((PLANES * ROWS, COLS), f32),
            in_specs=[anywhere] * 4,
            out_specs=pl.BlockSpec(memory_space=pltpu.VMEM),
            scratch_shapes=[
                pltpu.VMEM((PLANES * ROWS, COLS), f32),
                pltpu.VMEM((8 * ROWS, COLS), f32),
                pltpu.VMEM((fields * levels * sizes[2], eof_count), bf16),
                pltpu.VMEM((members, deep * sizes[2], COLS), bf16),
                pltpu.VMEM((PLANES * ROWS, deep * sizes[2]), bf16),
                pltpu.VMEM((PLANES * ROWS, members * COLS), f32),
                pltpu.VMEM((EXT, 5, 8, 2 * COLS), f32),
                pltpu.VMEM((EXT, 4, 8, 2 * COLS), f32),
                pltpu.VMEM((ROWS, WIDE, COLS), bf16),
                pltpu.VMEM((WIDE, COLS), bf16),
                pltpu.VMEM((DEPTH, WIDE, COLS), bf16),
                pltpu.VMEM((DEPTH, WIDE, COLS), bf16),
                pltpu.VMEM((6, WIDE, COLS), bf16),
                pltpu.VMEM((ROWS, PLANES, COLS), bf16),
                pltpu.VMEM((PLANES, COLS), bf16),
                pltpu.VMEM((DEPTH, PLANES, COLS), bf16),
                pltpu.VMEM((DEPTH, PLANES, COLS), bf16),
                pltpu.VMEM((6, PLANES, COLS), bf16),
                pltpu.SemaphoreType.DMA((5,)),
                pltpu.SemaphoreType.DMA((20,)),
                pltpu.SemaphoreType.DMA((20,)),
            ],
            compiler_params=pltpu.CompilerParams(
                collective_id=0, has_side_effects=True, vmem_limit_bytes=32 * 1024 * 1024
            ),
            name="covariance",
        )(
            panels.reshape(members, deep, columns),
            eof_basis.reshape(-1, eof_count),
            control.reshape(-1, COLS),
            coefficients.reshape(-1, COLS),
        )
        return out.reshape(control.shape)

    in_specs = (
        P(None, None, "gz", "gy", "gx"),
        P(),
        P(None, None, "gy", ("gx", "gz")),
        P(None, "gy", ("gx", "gz")),
    )
    return jax.shard_map(
        per_device,
        mesh=mesh,
        in_specs=in_specs,
        out_specs=P(None, None, "gy", ("gx", "gz")),
        check_vma=False,
    )
```

time: 432 us -> 63.6 us (0.15); the launches traced: 427 us -> 63.4 us
  starting transfers between devices: 214 us -> 0 us
  waiting for transfers between devices: 142 us -> 0 us
  Pallas kernels: 0 us -> 59.9 us
  local copies, waits for them, and re-layouts: 47.5 us -> 3.45 us
  other arithmetic: 21.6 us -> 0 us
    ppermute x52 -> x0, starting transfers between devices: 211 us -> none  [the longest x26 118 us: padded_2(): lax.ppermute(tail, axis, [(i, (i + 1) % count) for i in range(ends)])]
    ppermute x52 -> x0, waiting for transfers between devices: 142 us -> none  [the longest x26 115 us: padded_2(): lax.ppermute(head, axis, [((i + 1) % count, i) for i in range(ends)])]
    pallas_call x0 -> x1, Pallas kernels: none -> 59.9 us  [per_device(): pl.pallas_call(functools.partial(kernel, sizes), out_shape=jax.ShapeDtype...]
    unnamed x7 -> x8, local copies, waits for them, and re-layouts: 32.9 us -> 3.45 us
    all_to_all x1 -> x0, local copies, waits for them, and re-layouts: 11.6 us -> none  [per_device(): lax.all_to_all(panels, 'gz', split_axis=4, concat_axis=2, tiled=True)]
    add x24 -> x0, other arithmetic: 8.54 us -> none  [the longest x12 4.55 us: divergence(): coeffs[0, :-1, :-1] * east_diff + coeffs[1, :-1, :-1] * north_diff]
    mul x9 -> x0, other arithmetic: 5.22 us -> none  [the longest x7 3.72 us: adjoint_section(): coeffs[3] * padded]
    concatenate x13 -> x0, other arithmetic: 4.74 us -> none  [padded_2(): jnp.concatenate([lax.ppermute(tail, axis, [(i, (i + 1) % count) for i in...]
  transfers between devices with their start and end apart: 53 -> 0, of which waited for: 41 -> 0; matrix products, arithmetic and copies ran while one was open for 7% -> 0% of each run, Pallas kernels for 0% -> 0%
where the time goes in v1:
time: 63.6 us; the launch traced here: 63.4 us
  Pallas kernels  59.9 us (94%)
  local copies, waits for them, and re-layouts  3.45 us (5%)
    pallas_call x1, Pallas kernels, per_device(): pl.pallas_call(functools.partial(kernel, sizes), out_shape=jax.ShapeDtype...  59.9 us
    unnamed x8, local copies, waits for them, and re-layouts  3.45 us

profile of v1, /device:TPU:56, one launch (start us, length us, event | category | flops | bytes accessed | tf_op | source)
XLA Modules:
  0.0 63.4 jit_solution(6548429212167075466)
XLA Ops:
  0.0 0.0 copy-start.2
  0.0 0.8 %copy.5 = bf16[4,16,10]{2,1,0:T(8,128)(2,1)S(1)} copy(bf16[4,16,10]{1,0,2:T(4,128)(2,1)} %param.5) | data formatting | bytes 2560 | tf_op args[1]
  0.8 0.0 copy-done.2
  0.8 0.0 copy-start
  0.8 1.0 %copy-done = bf16[4,4,4,8,512]{4,3,2,1,0:T(8,128)(2,1)S(1)} copy-done((bf16[4,4,4,8,512]{4,3,2,1,0:T(8,128)(2,1)S(1)}, bf16[4,4,4,8,512]{4,3,2,1,0:T(8,128)(2,1)}, u32[]{:S(2)}) %copy-start) | copy-done | bytes 524312
  1.9 0.0 copy-start.1
  1.9 0.9 %copy-done.1 = f32[4,10,8,128]{3,2,1,0:T(8,128)S(1)} copy-done((f32[4,10,8,128]{3,2,1,0:T(8,128)S(1)}, f32[4,10,8,128]{3,2,1,0:T(8,128)}, u32[]{:S(2)}) %copy-start.1) | copy-done | bytes 163864
  2.8 59.9 %covariance.1 = f32[320,128]{1,0:T(8,128)S(1)} custom-call(bf16[4,128,512]{2,1,0:T(8,128)(2,1)S(1)} %bitcast.6, bf16[64,10]{1,0:T(8,128)(2,1)S(1)} %bitcast.8, f32[320,128]{1,0:T(8,128)S(1)} %bitcast.7, f32[32,128]{1,0:T(8,128)S(1)} %bitcast.9), custom_call_target="tpu_custom_call" | custom-call | tf_op jit(solution)/shard_map/covariance/pallas_call | solution.py:323
  62.7 0.7 %copy.7 = f32[4,10,8,128]{3,2,1,0:T(8,128)} copy(f32[4,10,8,128]{3,2,1,0:T(8,128)S(1)} %bitcast.5) | data formatting | bytes 327680
Async XLA Ops:
  0.0 0.8 %copy-start.2 = (f32[4,8,128]{2,1,0:T(8,128)S(1)}, f32[4,8,128]{2,1,0:T(8,128)}, u32[]{:S(2)}) copy-start(f32[4,8,128]{2,1,0:T(8,128)} %param.7) | copy-start | bytes 49156
  0.8 1.0 %copy-start = (bf16[4,4,4,8,512]{4,3,2,1,0:T(8,128)(2,1)S(1)}, bf16[4,4,4,8,512]{4,3,2,1,0:T(8,128)(2,1)}, u32[]{:S(2)}) copy-start(bf16[4,4,4,8,512]{4,3,2,1,0:T(8,128)(2,1)} %param.4) | copy-start | bytes 1572868
  1.9 0.9 %copy-start.1 = (f32[4,10,8,128]{3,2,1,0:T(8,128)S(1)}, f32[4,10,8,128]{3,2,1,0:T(8,128)}, u32[]{:S(2)}) copy-start(f32[4,10,8,128]{3,2,1,0:T(8,128)} %param.6) | copy-start | bytes 491524

commit v2 on v1

v2 whole, which is shorter than its diff:
```python
import functools

import jax
import jax.numpy as jnp
from jax import lax
from jax.experimental import pallas as pl
from jax.experimental.pallas import tpu as pltpu
from jax.sharding import PartitionSpec as P

STEPS = 6
TIME_STEP = 0.09
ROWS = 8
COLS = 128
DEPTH = STEPS
EXT = ROWS + 2 * DEPTH
SLOT = COLS // ROWS
HALF = SLOT // 2
PLANES = 40
GROUPS = PLANES // 8
LAG = 2
CHUNKS_A = ((0, 2), (2, 4), (4, 6))
CHUNKS_B = ((0, 2), (2, 4), (4, 5))
MESH = pl.DeviceIdType.MESH


def diffuse(grid, coef, group, forward):
    level = [{} for _ in range(STEPS + 1)]
    below = [None] * STEPS
    weighted = [{} for _ in range(STEPS)]

    def source(k, r):
        if r not in weighted[k]:
            weighted[k][r] = level[k][r] if forward else coef[r, 3] * level[k][r]
        return weighted[k][r]

    def update(k, r):
        here, above = source(k, r), source(k, r + 1)
        east = pltpu.roll(here, 2 * COLS - 1, 1) - here
        north = above - here
        kxy = coef[r, 1]
        flux_north = kxy * east + coef[r, 2] * north
        if r > k:
            flux_east = coef[r, 0] * east + kxy * north
            div = (flux_east - pltpu.roll(flux_east, 1, 1)) + (flux_north - below[k])
            old = level[k][r]
            new = old + coef[r, 3] * div if forward else old + div
            if k == STEPS - 1:
                grid[group, r] = new
            else:
                level[k + 1][r] = new
        below[k] = flux_north

    level[0][0] = grid[group, 0]
    for top in range(1, EXT + LAG * STEPS):
        if top < EXT:
            level[0][top] = grid[group, top]
        for k in range(STEPS):
            r = top - 1 - LAG * k
            if k <= r <= EXT - 2 - k:
                update(k, r)


def kernel(
    sizes,
    panels_hbm,
    eof_hbm,
    control_hbm,
    coef_hbm,
    out_ref,
    control,
    coef_in,
    eof,
    basis,
    panel,
    weight,
    projected,
    grid,
    coef,
    tile_a,
    edge_a,
    north_a,
    south_a,
    side_a,
    tile_b,
    edge_b,
    north_b,
    south_b,
    side_b,
    local_sem,
    send_sem,
    recv_sem,
):
    count_x, count_y, count_z = sizes
    gx, gy, gz = lax.axis_index("gx"), lax.axis_index("gy"), lax.axis_index("gz")
    place = gx * count_z + gz
    total = count_x * count_z
    east = lax.rem(place + 1, total)
    west = lax.rem(place + total - 1, total)
    up = lax.rem(gy + 1, count_y)
    down = lax.rem(gy + count_y - 1, count_y)

    def at(column, row):
        return (column // count_z, row, lax.rem(column, count_z))

    sides = [at(east, gy), at(west, gy), at(east, up), at(west, up), at(east, down), at(west, down)]
    peers = [(gx, gy, lax.rem(gz + d, count_z)) for d in range(1, count_z)]
    north_id, south_id = at(place, up), at(place, down)

    barrier = pltpu.get_barrier_semaphore()
    partners = sides + [north_id, south_id] + peers
    for partner in partners:
        pl.semaphore_signal(barrier, inc=1, device_id=partner, device_id_type=MESH)

    copies = [
        pltpu.make_async_copy(control_hbm, control, local_sem.at[0]),
        pltpu.make_async_copy(coef_hbm, coef_in.at[pl.ds(0, 32)], local_sem.at[1]),
        pltpu.make_async_copy(coef_hbm, coef_in.at[pl.ds(32, 32)], local_sem.at[2]),
        pltpu.make_async_copy(eof_hbm, eof, local_sem.at[3]),
    ]
    for copy in copies:
        copy.start()
    levels = panel.shape[1] // count_z
    mine = pl.ds(pl.multiple_of(gz * levels, levels), levels)
    own_panel = pltpu.make_async_copy(
        panels_hbm.at[:, :, pl.ds(pl.multiple_of(gz * COLS, COLS), COLS)],
        panel.at[:, mine, :],
        local_sem.at[4],
    )
    own_panel.start()

    lane = lax.broadcasted_iota(jnp.int32, (8, COLS), 1)
    first_half = (lane & (SLOT - 1)) < HALF
    sub8 = lax.broadcasted_iota(jnp.int32, (8, COLS), 0)
    slots = [(lane >= SLOT * y) & (lane < SLOT * (y + 1)) for y in range(ROWS)]

    def slotted(edges, y, blocks):
        for g, block in enumerate(blocks):
            shifted = pltpu.roll(block, SLOT * y + HALF, 1)
            edges[g] = shifted if edges[g] is None else jnp.where(slots[y], shifted, edges[g])

    def pack_edges(edges, edge):
        for pair in range(0, len(edges), 2):
            one = edges[pair]
            two = edges[pair + 1] if pair + 1 < len(edges) else one
            easting = jnp.where(first_half, one, pltpu.roll(two, HALF, 1))
            westing = jnp.where(first_half, pltpu.roll(one, COLS - HALF, 1), two)
            edge[0, pair // 2] = easting.astype(jnp.bfloat16)
            edge[1, pair // 2] = westing.astype(jnp.bfloat16)

    for copy in copies[:3]:
        copy.wait()
    edges = [None] * (GROUPS + 1)
    for y in range(ROWS):
        fields = control[pl.ds(y, PLANES, stride=ROWS), :]
        entries = coef_in[pl.ds(y, 8, stride=ROWS), :]
        high = entries.astype(jnp.bfloat16).astype(jnp.float32)
        blocks = [jnp.where(sub8 < 4, high, entries - high)]
        blocks += [fields[8 * g : 8 * g + 8] for g in range(GROUPS)]
        for g, block in enumerate(blocks):
            tile_a[g, y] = block.astype(jnp.bfloat16)
        slotted(edges, y, blocks)
    pack_edges(edges, edge_a)

    def exchange(first, chunks, tile, edge, north, south, side):
        moves = [(edge.at[k % 2], side.at[k], sides[k]) for k in range(6)]
        for a, b in chunks:
            groups = pl.ds(a, b - a)
            moves.append((tile.at[groups, pl.ds(ROWS - DEPTH, DEPTH)], south.at[groups], north_id))
            moves.append((tile.at[groups, pl.ds(0, DEPTH)], north.at[groups], south_id))
        return [
            pltpu.make_async_remote_copy(
                src_ref=source,
                dst_ref=target,
                send_sem=send_sem.at[first + k],
                recv_sem=recv_sem.at[first + k],
                device_id=device,
                device_id_type=MESH,
            )
            for k, (source, target, device) in enumerate(moves)
        ]

    pl.semaphore_wait(barrier, len(partners))
    halo_a = exchange(0, CHUNKS_A, tile_a, edge_a, north_a, south_a, side_a)
    for copy in halo_a:
        copy.start()
    sent_panels = []
    for d in range(1, count_z):
        peer = lax.rem(gz + d, count_z)
        copy = pltpu.make_async_remote_copy(
            src_ref=panels_hbm.at[:, :, pl.ds(pl.multiple_of(peer * COLS, COLS), COLS)],
            dst_ref=panel.at[:, mine, :],
            send_sem=send_sem.at[31 + d],
            recv_sem=recv_sem.at[31 + d],
            device_id=peers[d - 1],
            device_id_type=MESH,
        )
        copy.start()
        sent_panels.append(copy)

    def put_coef(row, start, entries):
        for k in range(4):
            scale = TIME_STEP if k == 3 else 1.0
            coef[row, k, :, start : start + COLS] = jnp.broadcast_to(
                scale * entries[k : k + 1], (8, COLS)
            )

    for y in range(ROWS):
        fields = control[pl.ds(y, PLANES, stride=ROWS), :]
        for g in range(GROUPS):
            grid[g, DEPTH + y, :, 0:COLS] = fields[8 * g : 8 * g + 8]
        put_coef(DEPTH + y, 0, coef_in[pl.ds(y, 8, stride=ROWS), :])

    copies[3].wait()
    count_e, count_f, count_l = eof.shape
    for e in range(count_e):
        block = eof[e].astype(jnp.float32)
        for f in range(count_f):
            basis[f * count_e + e : f * count_e + e + 1, :] = block[f : f + 1]
    plane = lax.broadcasted_iota(jnp.int32, (PLANES, 512), 0)
    field_of = jnp.zeros_like(plane)
    for f in range(1, count_f):
        field_of = field_of + jnp.where(plane >= f * count_e, 1, 0)
    spot = lax.broadcasted_iota(jnp.int32, (PLANES, 512), 1)
    same_field = field_of == (lax.shift_right_logical(spot, 5) & 3)
    level_row = lax.broadcasted_iota(jnp.int32, (count_l, 512), 0)
    level_spot = lax.broadcasted_iota(jnp.int32, (count_l, 512), 1)
    level_of = 4 * lax.shift_right_logical(level_spot, 7) + (lax.shift_right_logical(level_spot, 3) & 3)
    repeat = jnp.where(level_row == level_of, 1.0, 0.0).astype(jnp.bfloat16)
    spread = jnp.dot(basis[...].astype(jnp.bfloat16), repeat, preferred_element_type=jnp.float32)
    spread = jnp.where(same_field, spread, 0.0)
    for pair in range(ROWS // 2):
        both = [jnp.where((spot & 7) == 2 * pair + k, spread, 0.0) for k in range(2)]
        weight[pl.ds(2 * PLANES * pair, 2 * PLANES), :] = jnp.concatenate(both, axis=0).astype(jnp.bfloat16)

    keep_north = jnp.where(gy < count_y - 1, 1.0, 0.0).astype(jnp.float32)
    keep_south = jnp.where(gy > 0, 1.0, 0.0).astype(jnp.float32)
    ranges = (
        (DEPTH, 0, 0, ROWS, None),
        (0, 2, ROWS - DEPTH, DEPTH, keep_south),
        (DEPTH + ROWS, 4, 0, DEPTH, keep_north),
    )

    def edge_rows(side, group):
        for start, k, slot, count, keep in ranges:
            from_west = side[k, group // 2].astype(jnp.float32)
            from_east = side[k + 1, group // 2].astype(jnp.float32)
            if group % 2 == 0:
                pack = jnp.where(first_half, from_west, pltpu.roll(from_east, HALF, 1))
            else:
                pack = jnp.where(first_half, pltpu.roll(from_west, COLS - HALF, 1), from_east)
            if keep is not None:
                pack = pack * keep
            for y in range(count):
                yield start + y, pltpu.roll(pack, COLS - HALF - SLOT * (y + slot), 1)

    def halo_rows(north, south, group):
        for y in range(DEPTH):
            yield y, south[group, y].astype(jnp.float32) * keep_south
            yield DEPTH + ROWS + y, north[group, y].astype(jnp.float32) * keep_north

    def joined(parts):
        return parts + pltpu.roll(parts, 4, 0)

    for copy in halo_a[:6]:
        copy.wait_recv()
    for row, block in edge_rows(side_a, 0):
        put_coef(row, COLS, joined(block))
    for g in range(GROUPS):
        for row, block in edge_rows(side_a, g + 1):
            grid[g, row, :, COLS:] = block
    for i, (a, b) in enumerate(CHUNKS_A):
        for copy in halo_a[6 + 2 * i : 8 + 2 * i]:
            copy.wait_recv()
        for g in range(a, b):
            for row, block in halo_rows(north_a, south_a, g):
                if g == 0:
                    put_coef(row, 0, joined(block))
                else:
                    grid[g - 1, row, :, 0:COLS] = block

        def step_a(g, carry):
            diffuse(grid, coef, g, False)
            return carry

        lax.fori_loop(max(a - 1, 0), b - 1, step_a, 0)

    own_panel.wait()
    for copy in sent_panels:
        copy.wait_recv()
    members = panel.shape[0]
    for m in range(0, members, 2):
        pair = jnp.concatenate([panel[m], panel[m + 1]], axis=1)
        projected[:, m * COLS : (m + 2) * COLS] = jnp.dot(
            weight[...], pair, preferred_element_type=jnp.float32
        )

    edges = [None] * GROUPS
    for y in range(ROWS):
        factor = jnp.concatenate([grid[g, DEPTH + y, :, 0:COLS] for g in range(GROUPS)], axis=0)
        row = None
        for m in range(members):
            term = projected[y * PLANES : (y + 1) * PLANES, m * COLS : (m + 1) * COLS]
            score = jnp.sum(term * factor, axis=0, keepdims=True) * (1.0 / (members - 1))
            row = term * score if row is None else row + term * score
        blocks = [row[8 * g : 8 * g + 8] for g in range(GROUPS)]
        for g, block in enumerate(blocks):
            grid[g, DEPTH + y, :, 0:COLS] = block
            tile_b[g, y] = block.astype(jnp.bfloat16)
        slotted(edges, y, blocks)
    pack_edges(edges, edge_b)

    first_b = 6 + 2 * len(CHUNKS_A)
    halo_b = exchange(first_b, CHUNKS_B, tile_b, edge_b, north_b, south_b, side_b)
    for copy in halo_b:
        copy.start()
    for copy in halo_b[:6]:
        copy.wait_recv()
    for g in range(GROUPS):
        for row, block in edge_rows(side_b, g):
            grid[g, row, :, COLS:] = block
    for i, (a, b) in enumerate(CHUNKS_B):
        for copy in halo_b[6 + 2 * i : 8 + 2 * i]:
            copy.wait_recv()
        for g in range(a, b):
            for row, block in halo_rows(north_b, south_b, g):
                grid[g, row, :, 0:COLS] = block

        def step_b(g, carry):
            diffuse(grid, coef, g, True)
            return carry

        lax.fori_loop(a, b, step_b, 0)
        for g in range(a, b):
            for y in range(ROWS):
                out_ref[pl.ds(8 * ROWS * g + y, 8, stride=ROWS), :] = grid[g, DEPTH + y, :, 0:COLS]
    for copy in halo_a + sent_panels + halo_b:
        copy.wait_send()


def solution(mesh):
    sizes = tuple(mesh.shape[name] for name in ("gx", "gy", "gz"))

    def per_device(panels, eof_basis, control, coefficients):
        members, fields, levels, rows, columns = panels.shape
        eof_count = eof_basis.shape[2]
        deep = fields * levels * rows
        f32, bf16 = jnp.float32, jnp.bfloat16
        anywhere = pl.BlockSpec(memory_space=pl.ANY)
        wide = GROUPS + 1
        pairs_a, pairs_b = wide // 2, (GROUPS + 1) // 2
        out = pl.pallas_call(
            functools.partial(kernel, sizes),
            out_shape=jax.ShapeDtypeStruct((PLANES * ROWS, COLS), f32),
            in_specs=[anywhere] * 4,
            out_specs=pl.BlockSpec(memory_space=pltpu.VMEM),
            scratch_shapes=[
                pltpu.VMEM((PLANES * ROWS, COLS), f32),
                pltpu.VMEM((8 * ROWS, COLS), f32),
                pltpu.VMEM((eof_count, fields, levels * sizes[2]), bf16),
                pltpu.VMEM((PLANES, levels * sizes[2]), f32),
                pltpu.VMEM((members, deep * sizes[2], COLS), bf16),
                pltpu.VMEM((PLANES * ROWS, deep * sizes[2]), bf16),
                pltpu.VMEM((PLANES * ROWS, members * COLS), f32),
                pltpu.VMEM((GROUPS, EXT, 8, 2 * COLS), f32),
                pltpu.VMEM((EXT, 4, 8, 2 * COLS), f32),
                pltpu.VMEM((wide, ROWS, 8, COLS), bf16),
                pltpu.VMEM((2, pairs_a, 8, COLS), bf16),
                pltpu.VMEM((wide, DEPTH, 8, COLS), bf16),
                pltpu.VMEM((wide, DEPTH, 8, COLS), bf16),
                pltpu.VMEM((6, pairs_a, 8, COLS), bf16),
                pltpu.VMEM((GROUPS, ROWS, 8, COLS), bf16),
                pltpu.VMEM((2, pairs_b, 8, COLS), bf16),
                pltpu.VMEM((GROUPS, DEPTH, 8, COLS), bf16),
                pltpu.VMEM((GROUPS, DEPTH, 8, COLS), bf16),
                pltpu.VMEM((6, pairs_b, 8, COLS), bf16),
                pltpu.SemaphoreType.DMA((5,)),
                pltpu.SemaphoreType.DMA((36,)),
                pltpu.SemaphoreType.DMA((36,)),
            ],
            compiler_params=pltpu.CompilerParams(
                collective_id=0, has_side_effects=True, vmem_limit_bytes=63 * 1024 * 1024
            ),
            name="covariance",
        )(
            panels.reshape(members, deep, columns),
            eof_basis.transpose(2, 0, 1),
            control.reshape(-1, COLS),
            coefficients.reshape(-1, COLS),
        )
        return out.reshape(control.shape)

    in_specs = (
        P(None, None, "gz", "gy", "gx"),
        P(),
        P(None, None, "gy", ("gx", "gz")),
        P(None, "gy", ("gx", "gz")),
    )
    return jax.shard_map(
        per_device,
        mesh=mesh,
        in_specs=in_specs,
        out_specs=P(None, None, "gy", ("gx", "gz")),
        check_vma=False,
    )
```

time: 63.6 us -> 53.2 us (0.84)
  Pallas kernels: 59.9 us -> 51.3 us
  local copies, waits for them, and re-layouts: 3.45 us -> 1.59 us
    pallas_call x1, Pallas kernels: 59.9 us -> 51.3 us  [per_device(): pl.pallas_call(functools.partial(kernel, sizes), out_shape=jax.ShapeDtype...]
    unnamed x8 -> x1, local copies, waits for them, and re-layouts: 3.45 us -> 1.59 us
where the time goes in v2:
time: 53.2 us; the launch traced here: 52.9 us
  Pallas kernels  51.3 us (96%)
  local copies, waits for them, and re-layouts  1.59 us (3%)
    pallas_call x1, Pallas kernels, per_device(): pl.pallas_call(functools.partial(kernel, sizes), out_shape=jax.ShapeDtype...  51.3 us
    unnamed x1, local copies, waits for them, and re-layouts  1.59 us

profile of v2, /device:TPU:56, one launch (start us, length us, event | category | flops | bytes accessed | tf_op | source)
XLA Modules:
  0.0 52.9 jit_solution(5743318836744294323)
XLA Ops:
  0.0 51.3 %covariance.1 = f32[320,128]{1,0:T(8,128)} custom-call(bf16[4,128,512]{2,1,0:T(8,128)(2,1)} %bitcast.6, bf16[10,4,16]{2,1,0:T(4,128)(2,1)} %bitcast.9, f32[320,128]{1,0:T(8,128)} %bitcast.7, f32[32,128]{1,0:T(8,128)} %bitcast.8), custom_call_target="tpu_custom_call" | custom-call | tf_op jit(solution)/shard_map/covariance/pallas_call | solution.py:351
  51.3 1.6 %copy.6 = f32[4,10,8,128]{3,2,1,0:T(8,128)} copy(f32[4,10,8,128]{3,2,1,0:T(8,128)} %bitcast.5) | data formatting | bytes 327680

commit v3 on v2

--- a/solution.py
+++ b/solution.py
@@ -18,19 +18,22 @@
 PLANES = 40
 GROUPS = PLANES // 8
 LAG = 2
-CHUNKS_A = ((0, 2), (2, 4), (4, 6))
-CHUNKS_B = ((0, 2), (2, 4), (4, 5))
+LINES = 7
+TALL = COLS + 16
+STRIDE = 24
+CHUNKS_A = ((0, 1), (1, 3), (3, 5))
+CHUNKS_B = ((0, GROUPS),)
 MESH = pl.DeviceIdType.MESH
 
 
-def diffuse(grid, coef, group, forward):
+def adjoint_steps(grid, coef, group):
     level = [{} for _ in range(STEPS + 1)]
     below = [None] * STEPS
     weighted = [{} for _ in range(STEPS)]
 
     def source(k, r):
         if r not in weighted[k]:
-            weighted[k][r] = level[k][r] if forward else coef[r, 3] * level[k][r]
+            weighted[k][r] = coef[r, 3] * level[k][r]
         return weighted[k][r]
 
     def update(k, r):
@@ -43,7 +46,7 @@
             flux_east = coef[r, 0] * east + kxy * north
             div = (flux_east - pltpu.roll(flux_east, 1, 1)) + (flux_north - below[k])
             old = level[k][r]
-            new = old + coef[r, 3] * div if forward else old + div
+            new = old + div
             if k == STEPS - 1:
                 grid[group, r] = new
             else:
@@ -58,6 +61,44 @@
             r = top - 1 - LAG * k
             if k <= r <= EXT - 2 - k:
                 update(k, r)
+
+
+def forward_steps(turned, flux, coef_t):
+    part = TALL // 3
+
+    def one_step(_, carry):
+        for c in range(3):
+            rows = pl.ds(part * c, part)
+            ahead = pl.ds(part * c + 1, part)
+            behind = pl.ds(8 + part * c - 1, part)
+            stored = pl.ds(8 + part * c, part)
+
+            def flux_of(g, here, above):
+                east = turned[g, ahead] - here
+                north = above - here
+                kxy = coef_t[1, g, rows]
+                return coef_t[0, g, rows] * east + kxy * north, kxy * east + coef_t[2, g, rows] * north
+
+            last = turned[LINES - 1, rows]
+            after_last = pltpu.roll(turned[0, rows], COLS - PLANES, 1)
+            last_east, last_north = flux_of(LINES - 1, last, after_last)
+            below = pltpu.roll(last_north, PLANES, 1)
+            here = turned[0, rows]
+            for g in range(LINES):
+                if g < LINES - 1:
+                    above = turned[g + 1, rows]
+                    flux_east, flux_north = flux_of(g, here, above)
+                else:
+                    flux_east, flux_north = last_east, last_north
+                flux[g, stored] = flux_east
+                turned[g, rows] = here + coef_t[3, g, rows] * (
+                    (flux_east - flux[g, behind]) + (flux_north - below)
+                )
+                below = flux_north
+                here = above
+        return carry
+
+    lax.fori_loop(0, STEPS, one_step, 0)
 
 
 def kernel(
@@ -76,6 +117,9 @@
     projected,
     grid,
     coef,
+    tile_c,
+    north_c,
+    south_c,
     tile_a,
     edge_a,
     north_a,
@@ -86,6 +130,11 @@
     north_b,
     south_b,
     side_b,
+    own_b,
+    turned,
+    flux,
+    coef_rows,
+    coef_t,
     local_sem,
     send_sem,
     recv_sem,
@@ -156,13 +205,22 @@
         high = entries.astype(jnp.bfloat16).astype(jnp.float32)
         blocks = [jnp.where(sub8 < 4, high, entries - high)]
         blocks += [fields[8 * g : 8 * g + 8] for g in range(GROUPS)]
-        for g, block in enumerate(blocks):
+        for g, block in enumerate(blocks[1:]):
             tile_a[g, y] = block.astype(jnp.bfloat16)
+        if y % 2 == 0:
+            even, even_high = entries, high
+        else:
+            both = jnp.where(sub8 < 4, even, entries)
+            tile_c[1 + y // 2] = both.astype(jnp.bfloat16)
+            if y in (1, ROWS - 1):
+                left = both - jnp.where(sub8 < 4, even_high, high)
+                tile_c[0 if y == 1 else 1 + ROWS // 2] = left.astype(jnp.bfloat16)
         slotted(edges, y, blocks)
     pack_edges(edges, edge_a)
 
-    def exchange(first, chunks, tile, edge, north, south, side):
+    def exchange(first, chunks, tile, edge, north, south, side, extra=()):
         moves = [(edge.at[k % 2], side.at[k], sides[k]) for k in range(6)]
+        moves += extra
         for a, b in chunks:
             groups = pl.ds(a, b - a)
             moves.append((tile.at[groups, pl.ds(ROWS - DEPTH, DEPTH)], south.at[groups], north_id))
@@ -180,7 +238,11 @@
         ]
 
     pl.semaphore_wait(barrier, len(partners))
-    halo_a = exchange(0, CHUNKS_A, tile_a, edge_a, north_a, south_a, side_a)
+    extra = [
+        (tile_c.at[pl.ds(1 + (ROWS - DEPTH) // 2, DEPTH // 2 + 1)], south_c, north_id),
+        (tile_c.at[pl.ds(0, DEPTH // 2 + 1)], north_c, south_id),
+    ]
+    halo_a = exchange(0, CHUNKS_A, tile_a, edge_a, north_a, south_a, side_a, extra)
     for copy in halo_a:
         copy.start()
     sent_panels = []
@@ -189,8 +251,8 @@
         copy = pltpu.make_async_remote_copy(
             src_ref=panels_hbm.at[:, :, pl.ds(pl.multiple_of(peer * COLS, COLS), COLS)],
             dst_ref=panel.at[:, mine, :],
-            send_sem=send_sem.at[31 + d],
-            recv_sem=recv_sem.at[31 + d],
+            send_sem=send_sem.at[33 + d],
+            recv_sem=recv_sem.at[33 + d],
             device_id=peers[d - 1],
             device_id_type=MESH,
         )
@@ -200,15 +262,22 @@
     def put_coef(row, start, entries):
         for k in range(4):
             scale = TIME_STEP if k == 3 else 1.0
-            coef[row, k, :, start : start + COLS] = jnp.broadcast_to(
-                scale * entries[k : k + 1], (8, COLS)
-            )
+            entry = scale * entries[k : k + 1]
+            coef[row, k, :, start : start + COLS] = jnp.broadcast_to(entry, (8, COLS))
+            coef_rows[STRIDE * k + row : STRIDE * k + row + 1, start : start + COLS] = entry
 
     for y in range(ROWS):
         fields = control[pl.ds(y, PLANES, stride=ROWS), :]
         for g in range(GROUPS):
             grid[g, DEPTH + y, :, 0:COLS] = fields[8 * g : 8 * g + 8]
         put_coef(DEPTH + y, 0, coef_in[pl.ds(y, 8, stride=ROWS), :])
+
+    turned[...] = jnp.zeros_like(turned)
+    flux[...] = jnp.zeros_like(flux)
+    for k in range(4):
+        first = STRIDE * k + EXT
+        coef_rows[first : STRIDE * (k + 1), :] = jnp.zeros((STRIDE - EXT, 2 * COLS), jnp.float32)
+    coef_rows[4 * STRIDE :, :] = jnp.zeros((COLS - 4 * STRIDE, 2 * COLS), jnp.float32)
 
     copies[3].wait()
     count_e, count_f, count_l = eof.shape
@@ -240,16 +309,18 @@
         (DEPTH + ROWS, 4, 0, DEPTH, keep_north),
     )
 
+    def edge_pack(side, group, k, keep):
+        from_west = side[k, group // 2].astype(jnp.float32)
+        from_east = side[k + 1, group // 2].astype(jnp.float32)
+        if group % 2 == 0:
+            pack = jnp.where(first_half, from_west, pltpu.roll(from_east, HALF, 1))
+        else:
+            pack = jnp.where(first_half, pltpu.roll(from_west, COLS - HALF, 1), from_east)
+        return pack if keep is None else pack * keep
+
     def edge_rows(side, group):
         for start, k, slot, count, keep in ranges:
-            from_west = side[k, group // 2].astype(jnp.float32)
-            from_east = side[k + 1, group // 2].astype(jnp.float32)
-            if group % 2 == 0:
-                pack = jnp.where(first_half, from_west, pltpu.roll(from_east, HALF, 1))
-            else:
-                pack = jnp.where(first_half, pltpu.roll(from_west, COLS - HALF, 1), from_east)
-            if keep is not None:
-                pack = pack * keep
+            pack = edge_pack(side, group, k, keep)
             for y in range(count):
                 yield start + y, pltpu.roll(pack, COLS - HALF - SLOT * (y + slot), 1)
 
@@ -261,28 +332,56 @@
     def joined(parts):
         return parts + pltpu.roll(parts, 4, 0)
 
-    for copy in halo_a[:6]:
+    for copy in halo_a[:8]:
         copy.wait_recv()
     for row, block in edge_rows(side_a, 0):
         put_coef(row, COLS, joined(block))
+    for half in range(DEPTH // 2):
+        lower = south_c[half].astype(jnp.float32)
+        upper = north_c[1 + half].astype(jnp.float32)
+        if half == DEPTH // 2 - 1:
+            lower = lower + south_c[half + 1].astype(jnp.float32)
+        if half == 0:
+            upper = upper + north_c[0].astype(jnp.float32)
+        lower, upper = lower * keep_south, upper * keep_north
+        for k in range(2):
+            put_coef(2 * half + k, 0, lower[4 * k : 4 * k + 4])
+            put_coef(DEPTH + ROWS + 2 * half + k, 0, upper[4 * k : 4 * k + 4])
     for g in range(GROUPS):
         for row, block in edge_rows(side_a, g + 1):
             grid[g, row, :, COLS:] = block
     for i, (a, b) in enumerate(CHUNKS_A):
-        for copy in halo_a[6 + 2 * i : 8 + 2 * i]:
+        for copy in halo_a[8 + 2 * i : 10 + 2 * i]:
             copy.wait_recv()
         for g in range(a, b):
             for row, block in halo_rows(north_a, south_a, g):
-                if g == 0:
-                    put_coef(row, 0, joined(block))
-                else:
-                    grid[g - 1, row, :, 0:COLS] = block
+                grid[g, row, :, 0:COLS] = block
 
         def step_a(g, carry):
-            diffuse(grid, coef, g, False)
+            adjoint_steps(grid, coef, g)
             return carry
 
-        lax.fori_loop(max(a - 1, 0), b - 1, step_a, 0)
+        lax.fori_loop(a, b, step_a, 0)
+
+
+    pick_row = lax.broadcasted_iota(jnp.int32, (COLS, LINES * COLS), 0)
+    pick_lane = lax.broadcasted_iota(jnp.int32, (COLS, LINES * COLS), 1)
+    line_of = lax.shift_right_logical(pick_lane, 7)
+    pick_lane = pick_lane & (COLS - 1)
+    block_of = jnp.where(pick_lane >= PLANES, 1, 0) + jnp.where(pick_lane >= 2 * PLANES, 1, 0)
+    wanted = jnp.where(pick_lane < 3 * PLANES, line_of + LINES * block_of, 2 * COLS)
+    own, beyond = coef_rows[:, 0:COLS].T, coef_rows[:, COLS:].T
+    rest = jnp.concatenate([beyond[COLS - 8 :], own, beyond[0:8]], axis=0)
+    parts = []
+    for _ in range(3):
+        parts.append(rest.astype(jnp.bfloat16))
+        rest = rest - parts[-1].astype(jnp.float32)
+    left = jnp.concatenate(parts, axis=1)
+    for k in range(4):
+        ones = jnp.where(pick_row - STRIDE * k == wanted, 1.0, 0.0).astype(jnp.bfloat16)
+        turn = jnp.dot(left, jnp.concatenate([ones] * 3, axis=0), preferred_element_type=jnp.float32)
+        for g in range(LINES):
+            coef_t[k, g] = turn[:, g * COLS : (g + 1) * COLS]
 
     own_panel.wait()
     for copy in sent_panels:
@@ -304,35 +403,51 @@
             row = term * score if row is None else row + term * score
         blocks = [row[8 * g : 8 * g + 8] for g in range(GROUPS)]
         for g, block in enumerate(blocks):
-            grid[g, DEPTH + y, :, 0:COLS] = block
+            own_b[g, y] = block
             tile_b[g, y] = block.astype(jnp.bfloat16)
         slotted(edges, y, blocks)
     pack_edges(edges, edge_b)
 
-    first_b = 6 + 2 * len(CHUNKS_A)
+    first_b = len(halo_a)
     halo_b = exchange(first_b, CHUNKS_B, tile_b, edge_b, north_b, south_b, side_b)
     for copy in halo_b:
         copy.start()
     for copy in halo_b[:6]:
         copy.wait_recv()
-    for g in range(GROUPS):
-        for row, block in edge_rows(side_b, g):
-            grid[g, row, :, COLS:] = block
-    for i, (a, b) in enumerate(CHUNKS_B):
-        for copy in halo_b[6 + 2 * i : 8 + 2 * i]:
-            copy.wait_recv()
-        for g in range(a, b):
-            for row, block in halo_rows(north_b, south_b, g):
-                grid[g, row, :, 0:COLS] = block
-
-        def step_b(g, carry):
-            diffuse(grid, coef, g, True)
-            return carry
-
-        lax.fori_loop(a, b, step_b, 0)
-        for g in range(a, b):
-            for y in range(ROWS):
-                out_ref[pl.ds(8 * ROWS * g + y, 8, stride=ROWS), :] = grid[g, DEPTH + y, :, 0:COLS]
+    lanes = lax.broadcasted_iota(jnp.int32, (8, COLS), 1)
+    spare = jnp.zeros((COLS - 3 * PLANES, COLS), jnp.float32)
+    packs = [edge_pack(side_b, g, k, keep) for k, keep in ((2, keep_south), (0, None), (4, keep_north)) for g in range(GROUPS)]
+    packs = jnp.concatenate(packs + [spare], axis=0).T
+    for east_side in range(2):
+        place_at = pl.ds(east_side * (TALL - 8), 8)
+
+        def piece(y):
+            first = SLOT * y + HALF * east_side
+            return packs[first : first + 8]
+
+        for g in range(DEPTH):
+            middle = jnp.where(lanes < 2 * PLANES, piece(1 + g), piece(g))
+            turned[g, place_at] = jnp.where(lanes < PLANES, piece(2 + g), middle)
+        turned[DEPTH, place_at] = jnp.where(lanes < PLANES, pltpu.roll(piece(0), COLS - PLANES, 1), piece(ROWS - 1))
+    main = pl.ds(8, COLS)
+    ends = [own_b[g, y] for y in (0, ROWS - 1) for g in range(GROUPS)]
+    ends.append(jnp.zeros((COLS - 2 * PLANES, COLS), jnp.float32))
+    turned[DEPTH, main] = jnp.concatenate(ends, axis=0).T
+    for copy in halo_b[6:]:
+        copy.wait_recv()
+    for line in range(DEPTH):
+        stack = [south_b[g, line].astype(jnp.float32) * keep_south for g in range(GROUPS)]
+        stack += [own_b[g, 1 + line] for g in range(GROUPS)]
+        stack += [north_b[g, line].astype(jnp.float32) * keep_north for g in range(GROUPS)]
+        turned[line, main] = jnp.concatenate(stack + [spare], axis=0).T
+    forward_steps(turned, flux, coef_t)
+    for line in range(LINES):
+        back = turned[line, main].T
+        if line < DEPTH:
+            out_ref[pl.ds(1 + line, PLANES, stride=ROWS), :] = back[PLANES : 2 * PLANES]
+        else:
+            out_ref[pl.ds(0, PLANES, stride=ROWS), :] = back[0:PLANES]
+            out_ref[pl.ds(ROWS - 1, PLANES, stride=ROWS), :] = back[PLANES : 2 * PLANES]
     for copy in halo_a + sent_panels + halo_b:
         copy.wait_send()
 
@@ -363,19 +478,27 @@
                 pltpu.VMEM((PLANES * ROWS, members * COLS), f32),
                 pltpu.VMEM((GROUPS, EXT, 8, 2 * COLS), f32),
                 pltpu.VMEM((EXT, 4, 8, 2 * COLS), f32),
-                pltpu.VMEM((wide, ROWS, 8, COLS), bf16),
+                pltpu.VMEM((ROWS // 2 + 2, 8, COLS), bf16),
+                pltpu.VMEM((DEPTH // 2 + 1, 8, COLS), bf16),
+                pltpu.VMEM((DEPTH // 2 + 1, 8, COLS), bf16),
+                pltpu.VMEM((GROUPS, ROWS, 8, COLS), bf16),
                 pltpu.VMEM((2, pairs_a, 8, COLS), bf16),
-                pltpu.VMEM((wide, DEPTH, 8, COLS), bf16),
-                pltpu.VMEM((wide, DEPTH, 8, COLS), bf16),
+                pltpu.VMEM((GROUPS, DEPTH, 8, COLS), bf16),
+                pltpu.VMEM((GROUPS, DEPTH, 8, COLS), bf16),
                 pltpu.VMEM((6, pairs_a, 8, COLS), bf16),
                 pltpu.VMEM((GROUPS, ROWS, 8, COLS), bf16),
                 pltpu.VMEM((2, pairs_b, 8, COLS), bf16),
                 pltpu.VMEM((GROUPS, DEPTH, 8, COLS), bf16),
                 pltpu.VMEM((GROUPS, DEPTH, 8, COLS), bf16),
                 pltpu.VMEM((6, pairs_b, 8, COLS), bf16),
+                pltpu.VMEM((GROUPS, ROWS, 8, COLS), f32),
+                pltpu.VMEM((LINES, TALL + 8, COLS), f32),
+                pltpu.VMEM((LINES, TALL + 8, COLS), f32),
+                pltpu.VMEM((COLS, 2 * COLS), f32),
+                pltpu.VMEM((4, LINES, TALL, COLS), f32),
                 pltpu.SemaphoreType.DMA((5,)),
-                pltpu.SemaphoreType.DMA((36,)),
-                pltpu.SemaphoreType.DMA((36,)),
+                pltpu.SemaphoreType.DMA((44,)),
+                pltpu.SemaphoreType.DMA((44,)),
             ],
             compiler_params=pltpu.CompilerParams(
                 collective_id=0, has_side_effects=True, vmem_limit_bytes=63 * 1024 * 1024

time: 53.2 us -> 50.5 us (0.949)
  Pallas kernels: 51.3 us -> 48.6 us
    pallas_call x1, Pallas kernels: 51.3 us -> 48.6 us  [per_device(): pl.pallas_call(functools.partial(kernel, sizes), out_shape=jax.ShapeDtype...]
where the time goes in v3:
time: 50.5 us; the launch traced here: 50.2 us
  Pallas kernels  48.6 us (96%)
  local copies, waits for them, and re-layouts  1.59 us (3%)
    pallas_call x1, Pallas kernels, per_device(): pl.pallas_call(functools.partial(kernel, sizes), out_shape=jax.ShapeDtype...  48.6 us
    unnamed x1, local copies, waits for them, and re-layouts  1.59 us

profile of v3, /device:TPU:56, one launch (start us, length us, event | category | flops | bytes accessed | tf_op | source)
XLA Modules:
  0.0 50.2 jit_solution(15581836880175952021)
XLA Ops:
  0.0 48.6 %covariance.1 = f32[320,128]{1,0:T(8,128)} custom-call(bf16[4,128,512]{2,1,0:T(8,128)(2,1)} %bitcast.6, bf16[10,4,16]{2,1,0:T(4,128)(2,1)} %bitcast.9, f32[320,128]{1,0:T(8,128)} %bitcast.7, f32[32,128]{1,0:T(8,128)} %bitcast.8), custom_call_target="tpu_custom_call" | custom-call | tf_op jit(solution)/shard_map/covariance/pallas_call | solution.py:466
  48.6 1.6 %copy.6 = f32[4,10,8,128]{3,2,1,0:T(8,128)} copy(f32[4,10,8,128]{3,2,1,0:T(8,128)} %bitcast.5) | data formatting | bytes 327680

commit v4 on v3

--- a/solution.py
+++ b/solution.py
@@ -196,6 +196,28 @@
             edge[0, pair // 2] = easting.astype(jnp.bfloat16)
             edge[1, pair // 2] = westing.astype(jnp.bfloat16)
 
+    members = panel.shape[0]
+    sent_panels = []
+
+    def send_panels(first, last, row, end):
+        some = pl.ds(first, last - first)
+        for d in range(1, count_z):
+            peer = lax.rem(gz + d, count_z)
+            spot = pl.ds(pl.multiple_of(gz * levels + row, 16), end - row)
+            copy = pltpu.make_async_remote_copy(
+                src_ref=panels_hbm.at[some, pl.ds(row, end - row), pl.ds(pl.multiple_of(peer * COLS, COLS), COLS)],
+                dst_ref=panel.at[some, spot, :],
+                send_sem=send_sem.at[33 + len(sent_panels)],
+                recv_sem=recv_sem.at[33 + len(sent_panels)],
+                device_id=peers[d - 1],
+                device_id_type=MESH,
+            )
+            copy.start()
+            sent_panels.append(copy)
+
+    pl.semaphore_wait(barrier, len(partners))
+    send_panels(0, 1, 0, 64)
+
     for copy in copies[:3]:
         copy.wait()
     edges = [None] * (GROUPS + 1)
@@ -237,7 +259,6 @@
             for k, (source, target, device) in enumerate(moves)
         ]
 
-    pl.semaphore_wait(barrier, len(partners))
     extra = [
         (tile_c.at[pl.ds(1 + (ROWS - DEPTH) // 2, DEPTH // 2 + 1)], south_c, north_id),
         (tile_c.at[pl.ds(0, DEPTH // 2 + 1)], north_c, south_id),
@@ -245,19 +266,8 @@
     halo_a = exchange(0, CHUNKS_A, tile_a, edge_a, north_a, south_a, side_a, extra)
     for copy in halo_a:
         copy.start()
-    sent_panels = []
-    for d in range(1, count_z):
-        peer = lax.rem(gz + d, count_z)
-        copy = pltpu.make_async_remote_copy(
-            src_ref=panels_hbm.at[:, :, pl.ds(pl.multiple_of(peer * COLS, COLS), COLS)],
-            dst_ref=panel.at[:, mine, :],
-            send_sem=send_sem.at[33 + d],
-            recv_sem=recv_sem.at[33 + d],
-            device_id=peers[d - 1],
-            device_id_type=MESH,
-        )
-        copy.start()
-        sent_panels.append(copy)
+    send_panels(0, 1, 64, levels)
+    send_panels(1, members, 0, levels)
 
     def put_coef(row, start, entries):
         for k in range(4):
@@ -386,7 +396,6 @@
     own_panel.wait()
     for copy in sent_panels:
         copy.wait_recv()
-    members = panel.shape[0]
     for m in range(0, members, 2):
         pair = jnp.concatenate([panel[m], panel[m + 1]], axis=1)
         projected[:, m * COLS : (m + 2) * COLS] = jnp.dot(

time: 50.5 us -> 49.6 us (0.982)
  the two profiles are of different devices: /device:TPU:56 before, /device:TPU:160 now
where the time goes in v4:
time: 49.6 us; the launch traced here: 49.4 us
  Pallas kernels  47.8 us (96%)
  local copies, waits for them, and re-layouts  1.59 us (3%)
    pallas_call x1, Pallas kernels, per_device(): pl.pallas_call(functools.partial(kernel, sizes), out_shape=jax.ShapeDtype...  47.8 us
    unnamed x1, local copies, waits for them, and re-layouts  1.59 us

profile of v4, /device:TPU:160, one launch (start us, length us, event | category | flops | bytes accessed | tf_op | source)
XLA Modules:
  0.0 49.4 jit_solution(16361995010886289743)
XLA Ops:
  0.0 47.8 %covariance.1 = f32[320,128]{1,0:T(8,128)} custom-call(bf16[4,128,512]{2,1,0:T(8,128)(2,1)} %bitcast.6, bf16[10,4,16]{2,1,0:T(4,128)(2,1)} %bitcast.9, f32[320,128]{1,0:T(8,128)} %bitcast.7, f32[32,128]{1,0:T(8,128)} %bitcast.8), custom_call_target="tpu_custom_call" | custom-call | tf_op jit(solution)/shard_map/covariance/pallas_call | solution.py:475
  47.8 1.6 %copy.6 = f32[4,10,8,128]{3,2,1,0:T(8,128)} copy(f32[4,10,8,128]{3,2,1,0:T(8,128)} %bitcast.5) | data formatting | bytes 327680

commit v5 on v4

--- a/solution.py
+++ b/solution.py
@@ -135,6 +135,7 @@
     flux,
     coef_rows,
     coef_t,
+    finished,
     local_sem,
     send_sem,
     recv_sem,
@@ -450,15 +451,24 @@
         stack += [north_b[g, line].astype(jnp.float32) * keep_north for g in range(GROUPS)]
         turned[line, main] = jnp.concatenate(stack + [spare], axis=0).T
     forward_steps(turned, flux, coef_t)
+    stores = []
+
+    def store(y, block):
+        finished[y] = block
+        stores.append(pltpu.make_async_copy(finished.at[y], out_ref.at[:, y, :], local_sem.at[5 + y]))
+        stores[-1].start()
+
     for line in range(LINES):
         back = turned[line, main].T
         if line < DEPTH:
-            out_ref[pl.ds(1 + line, PLANES, stride=ROWS), :] = back[PLANES : 2 * PLANES]
+            store(1 + line, back[PLANES : 2 * PLANES])
         else:
-            out_ref[pl.ds(0, PLANES, stride=ROWS), :] = back[0:PLANES]
-            out_ref[pl.ds(ROWS - 1, PLANES, stride=ROWS), :] = back[PLANES : 2 * PLANES]
+            store(0, back[0:PLANES])
+            store(ROWS - 1, back[PLANES : 2 * PLANES])
     for copy in halo_a + sent_panels + halo_b:
         copy.wait_send()
+    for copy in stores:
+        copy.wait()
 
 
 def solution(mesh):
@@ -474,9 +484,9 @@
         pairs_a, pairs_b = wide // 2, (GROUPS + 1) // 2
         out = pl.pallas_call(
             functools.partial(kernel, sizes),
-            out_shape=jax.ShapeDtypeStruct((PLANES * ROWS, COLS), f32),
+            out_shape=jax.ShapeDtypeStruct((PLANES, ROWS, COLS), f32),
             in_specs=[anywhere] * 4,
-            out_specs=pl.BlockSpec(memory_space=pltpu.VMEM),
+            out_specs=anywhere,
             scratch_shapes=[
                 pltpu.VMEM((PLANES * ROWS, COLS), f32),
                 pltpu.VMEM((8 * ROWS, COLS), f32),
@@ -505,7 +515,8 @@
                 pltpu.VMEM((LINES, TALL + 8, COLS), f32),
                 pltpu.VMEM((COLS, 2 * COLS), f32),
                 pltpu.VMEM((4, LINES, TALL, COLS), f32),
-                pltpu.SemaphoreType.DMA((5,)),
+                pltpu.VMEM((ROWS, PLANES, COLS), f32),
+                pltpu.SemaphoreType.DMA((5 + ROWS,)),
                 pltpu.SemaphoreType.DMA((44,)),
                 pltpu.SemaphoreType.DMA((44,)),
             ],

time: 49.6 us -> 49.6 us (level)
  no operation moved by 1% of the time
where the time goes in v5:
time: 49.6 us; the launch traced here: 49.4 us
  Pallas kernels  47.8 us (96%)
  local copies, waits for them, and re-layouts  1.59 us (3%)
    pallas_call x1, Pallas kernels, per_device(): pl.pallas_call(functools.partial(kernel, sizes), out_shape=jax.ShapeDtype...  47.8 us
    unnamed x1, local copies, waits for them, and re-layouts  1.59 us

profile of v5, /device:TPU:160, one launch (start us, length us, event | category | flops | bytes accessed | tf_op | source)
XLA Modules:
  0.0 49.4 jit_solution(423701813762411573)
XLA Ops:
  0.0 47.8 %covariance.1 = f32[40,8,128]{2,1,0:T(8,128)} custom-call(bf16[4,128,512]{2,1,0:T(8,128)(2,1)} %bitcast.6, bf16[10,4,16]{2,1,0:T(4,128)(2,1)} %bitcast.9, f32[320,128]{1,0:T(8,128)} %bitcast.7, f32[32,128]{1,0:T(8,128)} %bitcast.8), custom_call_target="tpu_custom_call" | custom-call | tf_op jit(solution)/shard_map/covariance/pallas_call | solution.py:485
  47.8 1.6 %copy.6 = f32[4,10,8,128]{3,2,1,0:T(8,128)} copy(f32[4,10,8,128]{3,2,1,0:T(8,128)} %bitcast.5) | data formatting | bytes 327680
